TPU v7x, 32 devices: a whole 2x2x4 slice. The times are simulated.
32 devices in a mesh: batch: 4 (over y, x), ctx: 8 (over z, core).
Axes of the slice: x: 2, y: 2, z: 4, core: 2. Of those that a mesh axis runs over, the one named last changes fastest.
Arguments:
- inputs: float32 [4, 1024, 2304], P('batch', 'ctx'), may hold values from -6 to 6
- block_order: int32 [4, 8], P('batch'), may hold values from 0 to 7, each once within a row
- cotangent: float32 [4, 1024, 2304], P('batch', 'ctx'), may hold values from -6 to 6
- attn_gain: bfloat16 [2304], P(('batch', 'ctx')), may hold values from 0.5 to 1.5
- post_attn_gain: bfloat16 [2304], P(('batch', 'ctx')), may hold values from 0.5 to 1.5
- ffn_gain: bfloat16 [2304], P(('batch', 'ctx')), may hold values from 0.5 to 1.5
- post_ffn_gain: bfloat16 [2304], P(('batch', 'ctx')), may hold values from 0.5 to 1.5
- query_weight: bfloat16 [2304, 2048], P(('batch', 'ctx')), may hold values from -0.5 to 0.5
- key_weight: bfloat16 [2304, 1024], P(('batch', 'ctx')), may hold values from -0.125 to 0.125
- value_weight: bfloat16 [2304, 1024], P(('batch', 'ctx')), may hold values from -0.125 to 0.125
- out_weight: bfloat16 [2048, 2304], P(('batch', 'ctx')), may hold values from -0.125 to 0.125
- gate_weight: bfloat16 [9216, 2304], P(('batch', 'ctx')), may hold values from -0.125 to 0.125
- up_weight: bfloat16 [9216, 2304], P(('batch', 'ctx')), may hold values from -0.125 to 0.125
- down_weight: bfloat16 [9216, 2304], P(('batch', 'ctx')), may hold values from -0.0625 to 0.0625
Outputs:
- output: float32 [4, 1024, 2304], P('batch', 'ctx')
- input_grad: float32 [4, 1024, 2304], P('batch', 'ctx')
- query_grad: float32 [2304, 2048], P(('batch', 'ctx'))
- key_grad: float32 [2304, 1024], P(('batch', 'ctx'))
- value_grad: float32 [2304, 1024], P(('batch', 'ctx'))
- out_grad: float32 [2048, 2304], P(('batch', 'ctx'))
- gate_grad: float32 [9216, 2304], P(('batch', 'ctx'))
- up_grad: float32 [9216, 2304], P(('batch', 'ctx'))
- down_grad: float32 [9216, 2304], P(('batch', 'ctx'))
- attn_gain_grad: float32 [2304], P(('batch', 'ctx'))
- post_attn_gain_grad: float32 [2304], P(('batch', 'ctx'))
- ffn_gain_grad: float32 [2304], P(('batch', 'ctx'))
- post_ffn_gain_grad: float32 [2304], P(('batch', 'ctx'))
Inputs may be any that keep to these rules, and one draw needn't show every extreme that they name: Each row of block_order names every block of 128 positions of its sequence exactly once.
All inputs are finite; a program needn't handle non-finite values.
Results may differ from a plain program's by a relative error of at most 0.02.
The roundings to bfloat16 on the way count: a program that leaves them out, or rounds other values in their place, can miss the bound.
Values may be sent and summed in bfloat16 or wider, within the bound.
No kernel may reach another device: no remote copies, remote signals or barrier semaphores. Data moves between devices by JAX's collectives and lax.ppermute only.
A program may use at most 512 MiB of HBM per device.

v0:
```python
import math

import jax
import jax.numpy as jnp
from jax import lax
from jax.sharding import PartitionSpec as P

HEADS = 8
KV_HEADS = 4
HEAD_DIM = 256


NORM_EPS = 1e-06
SOFT_CAP = 50.0


def normalize(values_in, gain_vec):
    inv_rms = lax.rsqrt(jnp.mean(values_in * values_in, axis=-1, keepdims=True) + NORM_EPS)
    return (values_in * inv_rms * gain_vec.astype(jnp.float32), inv_rms)


def norm_back(values_in, inv_rms, gain_vec, grad_in):
    scaled = values_in * inv_rms
    weighted = grad_in * gain_vec.astype(jnp.float32)
    grad_gain = jnp.sum(grad_in * scaled, axis=0)
    grad_values = inv_rms * (
        weighted - scaled * jnp.mean(weighted * scaled, axis=-1, keepdims=True)
    )
    return (grad_values, grad_gain)


def geglu(gate_val, up_val):
    return jax.nn.gelu(gate_val, approximate=True) * up_val


def rows_product(left_mat, right_mat):
    return lax.dot_general(
        left_mat, right_mat, (((1,), (1,)), ((), ())), preferred_element_type=jnp.float32
    )


def cols_product(left_mat, right_mat):
    return lax.dot_general(
        left_mat, right_mat, (((0,), (0,)), ((), ())), preferred_element_type=jnp.float32
    )


def key_positions(block_row, row_count, local_rows):
    row_index = jnp.arange(row_count, dtype=jnp.int32)
    which_block = row_index // local_rows
    block_ids = jnp.arange(block_row.shape[0], dtype=jnp.int32)
    matches = which_block[:, None] == block_ids[None, :]
    chosen = jnp.sum(jnp.where(matches, block_row[None, :], 0), axis=1)
    return chosen * local_rows + row_index % local_rows


def on_device(
    inputs,
    block_order,
    cotangent,
    attn_gain,
    post_attn_gain,
    ffn_gain,
    post_ffn_gain,
    query_weight,
    key_weight,
    value_weight,
    out_weight,
    gate_weight,
    up_weight,
    down_weight,
):
    local_rows = inputs.shape[1]
    features = inputs.shape[2]
    rows_x = inputs.reshape(local_rows, features)
    grad_y = cotangent.reshape(local_rows, features)
    block_row = block_order.reshape(-1)
    block_count = block_row.shape[0]
    seq_length = local_rows * block_count
    groups = KV_HEADS
    ratio = HEADS // KV_HEADS
    key_width = KV_HEADS * HEAD_DIM
    scale = 1.0 / math.sqrt(HEAD_DIM)
    ctx_index = lax.axis_index("ctx")
    own_block = jnp.sum(
        jnp.where(jnp.arange(block_count, dtype=jnp.int32) == ctx_index, block_row, 0)
    )
    query_pos = own_block * local_rows + jnp.arange(local_rows, dtype=jnp.int32)
    gathered = (
        lax.all_gather(query_weight, ("batch", "ctx"), axis=0, tiled=True),
        lax.all_gather(key_weight, ("batch", "ctx"), axis=0, tiled=True),
        lax.all_gather(value_weight, ("batch", "ctx"), axis=0, tiled=True),
        lax.all_gather(out_weight, ("batch", "ctx"), axis=0, tiled=True),
        lax.all_gather(attn_gain, ("batch", "ctx"), axis=0, tiled=True),
        lax.all_gather(post_attn_gain, ("batch", "ctx"), axis=0, tiled=True),
        lax.all_gather(ffn_gain, ("batch", "ctx"), axis=0, tiled=True),
        lax.all_gather(post_ffn_gain, ("batch", "ctx"), axis=0, tiled=True),
    )
    w_query, w_key, w_value, w_out, gain_one, gain_two, gain_three, gain_four = gathered
    normed, inv_one = normalize(rows_x, gain_one)
    normed_in = normed.astype(jnp.bfloat16)
    query = jnp.dot(normed_in, w_query, preferred_element_type=jnp.float32).astype(jnp.bfloat16)
    kv_local = jnp.concatenate(
        (
            jnp.dot(normed_in, w_key, preferred_element_type=jnp.float32),
            jnp.dot(normed_in, w_value, preferred_element_type=jnp.float32),
        ),
        axis=1,
    ).astype(jnp.bfloat16)
    q_heads = query.reshape(local_rows, groups, ratio, HEAD_DIM)
    shard_piece = lax.all_gather(kv_local, "ctx", axis=0, tiled=True)
    row_count = shard_piece.shape[0]
    key_heads = shard_piece[:, :key_width].reshape(row_count, groups, HEAD_DIM)
    value_heads = shard_piece[:, key_width:].reshape(row_count, groups, HEAD_DIM)
    key_pos = key_positions(block_row, row_count, local_rows)
    visible = key_pos[None, :] <= query_pos[:, None]
    tanh_val = jnp.tanh(
        jnp.einsum("tgrd,jgd->grtj", q_heads, key_heads, preferred_element_type=jnp.float32)
        * scale
        / SOFT_CAP
    )
    raw = jnp.where(visible, jnp.exp(SOFT_CAP * tanh_val), 0.0)
    accum = jnp.einsum(
        "grtj,jgd->tgrd", raw.astype(jnp.bfloat16), value_heads, preferred_element_type=jnp.float32
    )
    totals = jnp.sum(raw, axis=3)
    accum, totals, kv_all = (accum, totals, shard_piece)
    attended = (
        (accum / jnp.transpose(totals, (2, 0, 1))[..., None])
        .reshape(local_rows, HEADS * HEAD_DIM)
        .astype(jnp.bfloat16)
    )
    branch = jnp.dot(attended, w_out, preferred_element_type=jnp.float32)
    branch_normed, inv_two = normalize(branch, gain_two)
    middle = rows_x + branch_normed
    normed_m, inv_three = normalize(middle, gain_three)
    normed_mid = normed_m.astype(jnp.bfloat16)
    gate_piece = lax.all_gather(gate_weight, ("batch", "ctx"), axis=0, tiled=True)
    up_piece = lax.all_gather(up_weight, ("batch", "ctx"), axis=0, tiled=True)
    down_piece = lax.all_gather(down_weight, ("batch", "ctx"), axis=0, tiled=True)
    hidden_piece = geglu(
        rows_product(normed_mid, gate_piece), rows_product(normed_mid, up_piece)
    ).astype(jnp.bfloat16)
    ffn_out = jnp.dot(hidden_piece, down_piece, preferred_element_type=jnp.float32)
    ffn_normed, inv_four = normalize(ffn_out, gain_four)
    output = middle + ffn_normed
    grad_ffn, grad_four = norm_back(ffn_out, inv_four, gain_four, grad_y)
    grad_ffn_b = grad_ffn.astype(jnp.bfloat16)
    gate_piece = lax.all_gather(gate_weight, ("batch", "ctx"), axis=0, tiled=True)
    up_piece = lax.all_gather(up_weight, ("batch", "ctx"), axis=0, tiled=True)
    down_piece = lax.all_gather(down_weight, ("batch", "ctx"), axis=0, tiled=True)
    gate_act = rows_product(normed_mid, gate_piece)
    up_act = rows_product(normed_mid, up_piece)
    hidden_f, pull_back = jax.vjp(geglu, gate_act, up_act)
    grad_gate, grad_up = pull_back(rows_product(grad_ffn_b, down_piece))
    grad_gate_b = grad_gate.astype(jnp.bfloat16)
    grad_up_b = grad_up.astype(jnp.bfloat16)
    grad_nm = jnp.dot(grad_gate_b, gate_piece, preferred_element_type=jnp.float32) + jnp.dot(
        grad_up_b, up_piece, preferred_element_type=jnp.float32
    )
    rows_piece = lax.all_gather(normed_mid, ("batch", "ctx"), axis=0, tiled=True)
    cot_piece = lax.all_gather(grad_ffn_b, ("batch", "ctx"), axis=0, tiled=True)
    gate_act = rows_product(rows_piece, gate_weight)
    up_act = rows_product(rows_piece, up_weight)
    hidden_f, pull_back = jax.vjp(geglu, gate_act, up_act)
    grad_gate, grad_up = pull_back(rows_product(cot_piece, down_weight))
    gate_acc = cols_product(grad_gate.astype(jnp.bfloat16), rows_piece)
    up_acc = cols_product(grad_up.astype(jnp.bfloat16), rows_piece)
    down_acc = cols_product(hidden_f.astype(jnp.bfloat16), cot_piece)
    grad_mid_part, grad_three = norm_back(middle, inv_three, gain_three, grad_nm)
    grad_mid = grad_y + grad_mid_part
    grad_branch, grad_two = norm_back(branch, inv_two, gain_two, grad_mid)
    grad_branch_b = grad_branch.astype(jnp.bfloat16)
    out_term = cols_product(attended, grad_branch_b)
    grad_att = rows_product(grad_branch_b, w_out).astype(jnp.bfloat16)
    ga_heads = grad_att.reshape(local_rows, groups, ratio, HEAD_DIM)
    at_heads = attended.reshape(local_rows, groups, ratio, HEAD_DIM)
    delta = jnp.transpose(
        jnp.sum(ga_heads.astype(jnp.float32) * at_heads.astype(jnp.float32), axis=3), (1, 2, 0)
    )
    key_all = kv_all[:, :key_width].reshape(seq_length, groups, HEAD_DIM)
    value_all = kv_all[:, key_width:].reshape(seq_length, groups, HEAD_DIM)
    key_pos = key_positions(block_row, seq_length, local_rows)
    visible = key_pos[None, :] <= query_pos[:, None]
    tanh_val = jnp.tanh(
        jnp.einsum("tgrd,jgd->grtj", q_heads, key_all, preferred_element_type=jnp.float32)
        * scale
        / SOFT_CAP
    )
    prob = jnp.where(visible, jnp.exp(SOFT_CAP * tanh_val) / totals[..., None], 0.0)
    dprob = jnp.einsum("tgrd,jgd->grtj", ga_heads, value_all, preferred_element_type=jnp.float32)
    grad_z = (prob * (dprob - delta[..., None]) * (1.0 - tanh_val * tanh_val) * scale).astype(
        jnp.bfloat16
    )
    grad_query = (
        jnp.einsum("grtj,jgd->tgrd", grad_z, key_all, preferred_element_type=jnp.float32)
        .reshape(local_rows, HEADS * HEAD_DIM)
        .astype(jnp.bfloat16)
    )
    key_terms = jnp.einsum(
        "grtj,tgrd->jgd", grad_z, q_heads, preferred_element_type=jnp.float32
    ).reshape(seq_length, key_width)
    value_terms = jnp.einsum(
        "grtj,tgrd->jgd", prob.astype(jnp.bfloat16), ga_heads, preferred_element_type=jnp.float32
    ).reshape(seq_length, key_width)
    kv_terms = jnp.concatenate((key_terms, value_terms), axis=1)
    kv_own = lax.psum_scatter(kv_terms.astype(jnp.bfloat16), "ctx", scatter_dimension=0, tiled=True)
    grad_keys = kv_own[:, :key_width]
    grad_values = kv_own[:, key_width:]
    query_term = cols_product(normed_in, grad_query)
    key_term = cols_product(normed_in, grad_keys)
    value_term = cols_product(normed_in, grad_values)
    grad_in = (
        rows_product(grad_query, w_query)
        + rows_product(grad_keys, w_key)
        + rows_product(grad_values, w_value)
    )
    grad_x_part, grad_one = norm_back(rows_x, inv_one, gain_one, grad_in)
    input_grad = grad_mid + grad_x_part
    summed = (
        lax.psum_scatter(query_term, ("batch", "ctx"), scatter_dimension=0, tiled=True),
        lax.psum_scatter(key_term, ("batch", "ctx"), scatter_dimension=0, tiled=True),
        lax.psum_scatter(value_term, ("batch", "ctx"), scatter_dimension=0, tiled=True),
        lax.psum_scatter(out_term, ("batch", "ctx"), scatter_dimension=0, tiled=True),
        lax.psum_scatter(grad_one, ("batch", "ctx"), scatter_dimension=0, tiled=True),
        lax.psum_scatter(grad_two, ("batch", "ctx"), scatter_dimension=0, tiled=True),
        lax.psum_scatter(grad_three, ("batch", "ctx"), scatter_dimension=0, tiled=True),
        lax.psum_scatter(grad_four, ("batch", "ctx"), scatter_dimension=0, tiled=True),
    )
    (
        query_grad,
        key_grad,
        value_grad,
        out_grad,
        attn_gain_grad,
        post_attn_gain_grad,
        ffn_gain_grad,
        post_ffn_gain_grad,
    ) = summed
    return (
        output.reshape(1, local_rows, features),
        input_grad.reshape(1, local_rows, features),
        query_grad,
        key_grad,
        value_grad,
        out_grad,
        gate_acc,
        up_acc,
        down_acc,
        attn_gain_grad,
        post_attn_gain_grad,
        ffn_gain_grad,
        post_ffn_gain_grad,
    )


def solution(mesh):
    return jax.shard_map(
        on_device,
        mesh=mesh,
        in_specs=(
            P("batch", "ctx", None),
            P("batch", None),
            P("batch", "ctx", None),
            P(("batch", "ctx")),
            P(("batch", "ctx")),
            P(("batch", "ctx")),
            P(("batch", "ctx")),
            P(("batch", "ctx"), None),
            P(("batch", "ctx"), None),
            P(("batch", "ctx"), None),
            P(("batch", "ctx"), None),
            P(("batch", "ctx"), None),
            P(("batch", "ctx"), None),
            P(("batch", "ctx"), None),
        ),
        out_specs=(
            P("batch", "ctx", None),
            P("batch", "ctx", None),
            P(("batch", "ctx"), None),
            P(("batch", "ctx"), None),
            P(("batch", "ctx"), None),
            P(("batch", "ctx"), None),
            P(("batch", "ctx"), None),
            P(("batch", "ctx"), None),
            P(("batch", "ctx"), None),
            P(("batch", "ctx")),
            P(("batch", "ctx")),
            P(("batch", "ctx")),
            P(("batch", "ctx")),
        ),
        check_vma=False,
    )
```

profile of v0, /device:TPU:0, one launch (start us, length us, event | category | flops | bytes accessed | tf_op | source)
XLA Modules:
  0.0 2215.7 jit_solution(690600870943740185)
XLA Ops:
  12.1 42.5 %all-reduce.9 = (bf16[2304]{0:T(1024)(128)(2,1)S(1)}, bf16[2304]{0:T(1024)(128)(2,1)S(1)}, bf16[2304]{0:T(1024)(128)(2,1)S(1)}, bf16[2304]{0:T(1024)(128)(2,1)S(1)}) all-reduce(bf16[2304]{0:T(1024)(128)(2,1)S(1)} %dynamic-update-slice, bf16[2304]{0:T(1024)(128)(2,1)S(1)} %dynamic-update-slice.1, ...), channel_id=1, replica_groups=mesh['batch'=4,'ctx'=8] {'batch','ctx'}, use_global_device_ids=true, to_apply=%add | all-reduce | flops 9216 | bytes 36864
  54.6 1.4 fusion.56
  56.6 1.6 multiply_convert_fusion.12
  58.2 19.2 all-gather.13.cloned.1.call-done
  77.4 3.1 convolution_convert_fusion.3
  80.5 61.8 %all-gather.11.cloned.1.call-done = bf16[2304,1024]{1,0:T(8,128)(2,1)} async-done(((bf16[72,1024]{1,0:T(8,128)(2,1)}), bf16[2304,1024]{1,0:T(8,128)(2,1)}) %all-gather.11.cloned.1.call-update) | async-done | bytes 4718608 | tf_op jit(solution)/shard_map/all_gather | solution.py:91
  142.4 3.1 convolution_convert_fusion.4
  152.1 39.6 %all-gather.15.cloned.1.call-done = bf16[1024,2048]{1,0:T(8,128)(2,1)} async-done(((bf16[128,2048]{1,0:T(8,128)(2,1)}), bf16[1024,2048]{1,0:T(8,128)(2,1)}) %all-gather.15.cloned.1.call-update) | async-done | bytes 4194320 | tf_op jit(solution)/shard_map/all_gather | solution.py:111
  191.7 4.7 fusion.115
  196.4 4.5 reshape.167
  200.8 4.3 copy.68
  205.1 4.5 reshape.166
  209.6 65.3 %all-gather.17.cloned.1.call-done = bf16[2304,2048]{1,0:T(8,128)(2,1)} async-done(((bf16[72,2048]{1,0:T(8,128)(2,1)}), bf16[2304,2048]{1,0:T(8,128)(2,1)}) %all-gather.17.cloned.1.call-update) | async-done | bytes 9437200 | tf_op jit(solution)/shard_map/all_gather | solution.py:90
  275.0 5.1 convolution_convert_fusion.1
  280.3 3.4 fusion.18
  283.8 1.9 copy-done.32
  285.7 1.6 divide_convert_fusion
  287.3 70.6 %all-gather.19.cloned.1.call-done = bf16[2048,2304]{1,0:T(8,128)(2,1)} async-done(((bf16[64,2304]{1,0:T(8,128)(2,1)}), bf16[2048,2304]{1,0:T(8,128)(2,1)}) %all-gather.19.cloned.1.call-update) | async-done | bytes 9437200 | tf_op jit(solution)/shard_map/all_gather | solution.py:93
  357.9 5.3 multiply_reduce_fusion.9
  365.3 231.1 %all-gather.23.cloned.1.call-done = bf16[9216,2304]{1,0:T(8,128)(2,1)} async-done(((bf16[288,2304]{1,0:T(8,128)(2,1)}), bf16[9216,2304]{1,0:T(8,128)(2,1)}) %all-gather.23.cloned.1.call-update) | async-done | bytes 42467344 | tf_op jit(solution)/shard_map/all_gather | solution.py:139
  596.4 22.3 %fusion.117 = f32[128,9216]{1,0:T(8,128)} fusion(bf16[128,2304]{1,0:T(8,128)(2,1)S(1)} %multiply_convert_fusion.11, bf16[9216,2304]{1,0:T(8,128)(2,1)} %all-gather.23.cloned.1.call-done), kind=kOutput, calls=%fused_computation.174 | convolution fusion | flops 5435817984 | bytes 47775744 | tf_op jit(solution)/shard_map/dot_general | solution.py:37
  618.7 215.9 %all-gather.21.cloned.1.call-done = bf16[9216,2304]{1,0:T(8,128)(2,1)} async-done(((bf16[288,2304]{1,0:T(8,128)(2,1)}), bf16[9216,2304]{1,0:T(8,128)(2,1)}) %all-gather.21.cloned.1.call-update) | async-done | bytes 42467344 | tf_op jit(solution)/shard_map/all_gather | solution.py:138
  834.6 22.4 %fusion.116 = f32[128,9216]{1,0:T(8,128)} fusion(bf16[128,2304]{1,0:T(8,128)(2,1)S(1)} %multiply_convert_fusion.11, bf16[9216,2304]{1,0:T(8,128)(2,1)} %all-gather.21.cloned.1.call-done), kind=kOutput, calls=%fused_computation.173 | convolution fusion | flops 5435817984 | bytes 47775744 | tf_op jit(solution)/shard_map/dot_general | solution.py:37
  857.0 215.8 %all-gather.25.cloned.1.call-done = bf16[9216,2304]{1,0:T(8,128)(2,1)} async-done(((bf16[288,2304]{1,0:T(8,128)(2,1)}), bf16[9216,2304]{1,0:T(8,128)(2,1)}) %all-gather.25.cloned.1.call-update) | async-done | bytes 42467344 | tf_op jit(solution)/shard_map/all_gather | solution.py:140
  1072.9 20.8 multiply_reduce_fusion.7
  1093.6 2.6 fusion.55
  1096.2 3.0 multiply_convert_fusion.10
  1099.2 21.7 fusion.118
  1120.9 21.8 fusion.25
  1142.7 25.3 %multiply_reduce_fusion = (f32[2304]{0:T(1024)}, f32[128]{0:T(128)S(1)}, f32[128,2304]{1,0:T(8,128)}) fusion(f32[128,2304]{1,0:T(8,128)S(1)} %get-tuple-element.31, f32[128]{0:T(128)} %copy-done.27, f32[2304]{0:T(1024)S(1)} %convert_element_type.99, f32[128,2304]{1,0:T(8,128)} %fusion.25, bf16[9216,2304]{1,0:T(8,128)(2,1)} %all-gather.23.cloned.1.call-done, ...), kind=kOutput, calls=%fused_computation.82 | convolution fusion | flops 5449676800 | bytes 55462912 | tf_op jit(solution)/shard_map/dot_general | solution.py:158
  1168.0 3.3 multiply_reduce_fusion.1
  1172.6 6.9 convolution_convert_fusion
  1181.7 4.0 bitcast_convert_fusion
  1186.1 2.7 fusion.15
  1188.8 1.3 copy-done.9
  1190.9 2.5 pad_maximum_fusion
  1193.4 6.5 copy.82
  1201.3 46.9 %reduce-scatter.16.cloned.1.call-done = bf16[128,2048]{1,0:T(8,128)(2,1)} async-done(((bf16[1024,2048]{1,0:T(8,128)(2,1)}), bf16[128,2048]{1,0:T(8,128)(2,1)}) %reduce-scatter.16.cloned.1.call-update) | async-done | bytes 524304
  1248.2 6.0 fusion.70
  1255.3 5.0 fusion.67
  1260.4 2.9 convolution_convert_fusion.2
  1263.4 8.2 fusion.62
  1271.7 8.0 fusion.120
  1279.7 93.9 %all-gather.29.cloned.1.call-done = bf16[4096,2304]{1,0:T(8,128)(2,1)} async-done(((bf16[128,2304]{1,0:T(8,128)(2,1)}), bf16[4096,2304]{1,0:T(8,128)(2,1)}) %all-gather.29.cloned.1.call-update) | async-done | bytes 18874384 | tf_op jit(solution)/shard_map/all_gather | solution.py:161
  1373.5 11.5 fusion.123
  1385.0 12.8 fusion.122
  1397.9 3.2 fusion.119
  1401.1 1.7 convolution_add_fusion.1
  1402.8 2.4 multiply_reduce_fusion.2
  1405.2 42.1 %all-reduce.8 = (f32[2304]{0:T(1024)}, f32[2304]{0:T(1024)}, f32[2304]{0:T(1024)}, f32[2304]{0:T(1024)}) all-reduce(f32[2304]{0:T(1024)} %get-tuple-element.19, f32[2304]{0:T(1024)} %get-tuple-element.17, f32[2304]{0:T(1024)} %get-tuple-element.15, f32[2304]{0:T(1024)} %get-tuple-element.13), channel_id=7, replica_groups=mesh['batch'=4,'ctx'=8] {'batch','ctx'}, use_global_device_ids=true, to_apply=%region_18.19.clone | all-reduce | flops 9216 | bytes 73728
  1447.4 1.3 dynamic-slice
  1448.7 1.3 dynamic-slice.1
  1449.9 1.3 dynamic-slice.2
  1451.2 1.3 dynamic-slice.3
  1453.1 1.3 add_bitcast_fusion
  1454.4 46.2 %all-gather.27.cloned.1.call-done = bf16[4096,2304]{1,0:T(8,128)(2,1)} async-done(((bf16[128,2304]{1,0:T(8,128)(2,1)}), bf16[4096,2304]{1,0:T(8,128)(2,1)}) %all-gather.27.cloned.1.call-update) | async-done | bytes 18874384 | tf_op jit(solution)/shard_map/all_gather | solution.py:162
  1500.6 13.3 fusion.121
  1513.9 16.9 fusion.21
  1530.8 11.3 fusion.22
  1542.1 21.0 fusion.23
  1563.1 78.3 %reduce-scatter.10.cloned.1.call-done = f32[72,1024]{1,0:T(8,128)} async-done(((f32[2304,1024]{1,0:T(8,128)}), f32[72,1024]{1,0:T(8,128)}) %reduce-scatter.10.cloned.1.call-update) | async-done | bytes 294928 | tf_op jit(solution)/shard_map/reduce_scatter | solution.py:222
  1641.4 141.7 %reduce-scatter.12.cloned.1.call-done = f32[72,1024]{1,0:T(8,128)} async-done(((f32[2304,1024]{1,0:T(8,128)}), f32[72,1024]{1,0:T(8,128)}) %reduce-scatter.12.cloned.1.call-update) | async-done | bytes 294928 | tf_op jit(solution)/shard_map/reduce_scatter | solution.py:223
  1783.0 212.6 %reduce-scatter.8.cloned.1.call-done = f32[72,2048]{1,0:T(8,128)} async-done(((f32[2304,2048]{1,0:T(8,128)}), f32[72,2048]{1,0:T(8,128)}) %reduce-scatter.8.cloned.1.call-update) | async-done | bytes 589840 | tf_op jit(solution)/shard_map/reduce_scatter | solution.py:221
  1995.7 213.0 %reduce-scatter.14.cloned.1.call-done = f32[64,2304]{1,0:T(8,128)} async-done(((f32[2048,2304]{1,0:T(8,128)}), f32[64,2304]{1,0:T(8,128)}) %reduce-scatter.14.cloned.1.call-update) | async-done | bytes 589840 | tf_op jit(solution)/shard_map/reduce_scatter | solution.py:224
  (158 shorter events, 21.4 us)
Async XLA Ops:
  7.2 70.2 %all-gather.13.cloned.1.call-start = ((), (), s32[]{:S(2)}) async-start(), calls=%async_computation.6 | async-start | bytes 4866048 | tf_op jit(solution)/shard_map/all_gather | solution.py:92
  7.9 134.4 %all-gather.11.cloned.1.call-start = ((), (), s32[]{:S(2)}) async-start(), calls=%async_computation.5 | async-start | bytes 4866048 | tf_op jit(solution)/shard_map/all_gather | solution.py:91
  8.7 183.0 %all-gather.15.cloned.1.call-start = ((), (), s32[]{:S(2)}) async-start(), calls=%async_computation.7 | async-start | bytes 4718592 | tf_op jit(solution)/shard_map/all_gather | solution.py:111
  54.6 1.5 copy-start.18
  56.1 0.5 copy-start.25
  145.5 5.0 copy-start.29
  146.4 128.6 %all-gather.17.cloned.1.call-start = ((), (), s32[]{:S(2)}) async-start(), calls=%async_computation.8 | async-start | bytes 9732096 | tf_op jit(solution)/shard_map/all_gather | solution.py:90
  146.9 211.0 %all-gather.19.cloned.1.call-start = ((), (), s32[]{:S(2)}) async-start(), calls=%async_computation.9 | async-start | bytes 9732096 | tf_op jit(solution)/shard_map/all_gather | solution.py:93
  147.5 448.9 %all-gather.23.cloned.1.call-start = ((), (), s32[]{:S(2)}) async-start(), calls=%async_computation.11 | async-start | bytes 43794432 | tf_op jit(solution)/shard_map/all_gather | solution.py:139
  148.1 686.5 %all-gather.21.cloned.1.call-start = ((), (), s32[]{:S(2)}) async-start(), calls=%async_computation.10 | async-start | bytes 43794432 | tf_op jit(solution)/shard_map/all_gather | solution.py:138
  148.8 924.0 %all-gather.25.cloned.1.call-start = ((), (), s32[]{:S(2)}) async-start(), calls=%async_computation.12 | async-start | bytes 43794432 | tf_op jit(solution)/shard_map/all_gather | solution.py:140
  149.6 1098.6 %reduce-scatter.16.cloned.1.call-start = ((), (), s32[]{:S(2)}) async-start(), calls=%async_computation.19 | async-start | bytes 4718592
  149.9 213.4 %copy-start.20 = (f32[2304]{0:T(1024)}, f32[2304]{0:T(1024)S(1)}, u32[]{:S(2)}) copy-start(f32[2304]{0:T(1024)S(1)} %convert_element_type.98) | copy-start | bytes 27652
  152.1 131.7 %copy-start.22 = (pred[128,1024]{0,1:T(8,128)(4,1)}, pred[128,1024]{0,1:T(8,128)(4,1)S(1)}, u32[]{:S(2)}) copy-start(pred[128,1024]{0,1:T(8,128)(4,1)S(1)} %broadcast_compare_fusion) | copy-start | bytes 393220
  280.3 3.5 copy-start.10
  280.3 5.4 copy-start.12
  283.8 2.0 copy-start.32
  283.8 3.5 copy-start.30
  287.3 75.9 %copy-start.6 = (bf16[128,4,2,256]{0,3,2,1:T(8,128)(2,1)}, bf16[128,4,2,256]{0,3,2,1:T(8,128)(2,1)S(1)}, u32[]{:S(2)}) copy-start(bf16[128,4,2,256]{0,3,2,1:T(8,128)(2,1)S(1)} %divide_convert_fusion) | copy-start | bytes 1572868
  357.9 6.3 copy-start
  363.2 1.0 copy-start.1
  364.6 0.5 copy-start.27
  365.3 469.3 %copy-start.5 = (bf16[128,2304]{1,0:T(8,128)(2,1)}, bf16[128,2304]{1,0:T(8,128)(2,1)S(1)}, u32[]{:S(2)}) copy-start(bf16[128,2304]{1,0:T(8,128)(2,1)S(1)} %multiply_convert_fusion.11) | copy-start | bytes 1769476
  857.0 236.6 %copy-start.24 = (f32[2304]{0:T(1024)S(1)}, f32[2304]{0:T(1024)}, u32[]{:S(2)}) copy-start(f32[2304]{0:T(1024)} %convert_element_type.102) | copy-start | bytes 27652
  1099.2 21.7 copy-start.8
  1142.7 25.3 %copy-start.21 = (f32[2304]{0:T(1024)S(1)}, f32[2304]{0:T(1024)}, u32[]{:S(2)}) copy-start(f32[2304]{0:T(1024)} %copy-done.20) | copy-start | bytes 27652
  1142.7 25.3 %copy-start.28 = (f32[128]{0:T(128)S(1)}, f32[128]{0:T(128)}, u32[]{:S(2)}) copy-start(f32[128]{0:T(128)} %copy-done.27) | copy-start | bytes 1540
  1168.0 4.3 copy-start.2
  1171.3 1.0 copy-start.3
  1172.6 7.9 copy-start.7
  1172.6 9.1 copy-start.23
  1172.6 9.1 copy-start.31
  1181.7 4.0 copy-start.13
  1181.7 4.0 copy-start.14
  1181.7 4.4 copy-start.33
  1186.1 4.0 copy-start.11
  1188.8 1.3 copy-start.9
  1199.9 173.6 %all-gather.29.cloned.1.call-start = ((), (), s32[]{:S(2)}) async-start(), calls=%async_computation.18 | async-start | bytes 19464192 | tf_op jit(solution)/shard_map/all_gather | solution.py:161
  1200.5 300.1 %all-gather.27.cloned.1.call-start = ((), (), s32[]{:S(2)}) async-start(), calls=%async_computation.17 | async-start | bytes 19464192 | tf_op jit(solution)/shard_map/all_gather | solution.py:162
  1201.2 440.2 %reduce-scatter.10.cloned.1.call-start = ((), (), s32[]{:S(2)}) async-start(), calls=%async_computation.14 | async-start | bytes 9732096 | tf_op jit(solution)/shard_map/reduce_scatter | solution.py:222
  1254.2 1.0 copy-start.15
  1254.2 528.8 %reduce-scatter.12.cloned.1.call-start = ((), (), s32[]{:S(2)}) async-start(), calls=%async_computation.15 | async-start | bytes 9732096 | tf_op jit(solution)/shard_map/reduce_scatter | solution.py:223
  1260.3 3.0 copy-start.19
  1260.3 3.0 copy-start.26
  1260.4 735.3 %reduce-scatter.8.cloned.1.call-start = ((), (), s32[]{:S(2)}) async-start(), calls=%async_computation.13 | async-start | bytes 19464192 | tf_op jit(solution)/shard_map/reduce_scatter | solution.py:221
  1271.6 937.0 %reduce-scatter.14.cloned.1.call-start = ((), (), s32[]{:S(2)}) async-start(), calls=%async_computation.16 | async-start | bytes 19464192 | tf_op jit(solution)/shard_map/reduce_scatter | solution.py:224
  1373.5 11.5 copy-start.17
  1373.5 24.3 %slice-start = ((s8[9437184]{0:T(1024)(128)(4,1)}), s8[4194304]{0:T(1024)(128)(4,1)S(1)}, s32[]{:S(2)}) async-start(s8[9437184]{0:T(1024)(128)(4,1)} %bitcast.141), calls=%async_computation.20 | async-start | bytes 8388608
  1373.5 24.3 %slice-start.1 = ((s8[9437184]{0:T(1024)(128)(4,1)}), s8[4194304]{0:T(1024)(128)(4,1)S(1)}, s32[]{:S(2)}) async-start(s8[9437184]{0:T(1024)(128)(4,1)} %bitcast.141), calls=%async_computation.21 | async-start | bytes 8388608
  1373.5 27.5 %slice-start.3 = ((s8[4718592]{0:T(1024)(128)(4,1)}), s8[4194304]{0:T(1024)(128)(4,1)S(1)}, s32[]{:S(2)}) async-start(s8[4718592]{0:T(1024)(128)(4,1)} %bitcast.143), calls=%async_computation.23 | async-start | bytes 8388608
  1373.5 29.2 %slice-start.5 = ((s8[4718592]{0:T(1024)(128)(4,1)}), s8[4194304]{0:T(1024)(128)(4,1)S(1)}, s32[]{:S(2)}) async-start(s8[4718592]{0:T(1024)(128)(4,1)} %bitcast.145), calls=%async_computation.25 | async-start | bytes 8388608
  1385.0 12.9 slice-start.2
  1385.0 16.1 slice-start.4
  1385.0 17.8 slice-start.6
  1401.1 1.7 copy-start.16
  1402.8 50.3 %copy-start.4 = (f32[128,2304]{1,0:T(8,128)S(1)}, f32[128,2304]{1,0:T(8,128)}, u32[]{:S(2)}) copy-start(f32[128,2304]{1,0:T(8,128)} %copy-done.3) | copy-start | bytes 3538948
  1500.6 30.2 %slice-start.7 = ((s8[18874368]{0:T(1024)(128)(4,1)}), s8[4194304]{0:T(1024)(128)(4,1)S(1)}, s32[]{:S(2)}) async-start(s8[18874368]{0:T(1024)(128)(4,1)} %bitcast.162), calls=%async_computation.27 | async-start | bytes 8388608
  1500.6 30.2 %slice-start.8 = ((s8[18874368]{0:T(1024)(128)(4,1)}), s8[4194304]{0:T(1024)(128)(4,1)S(1)}, s32[]{:S(2)}) async-start(s8[18874368]{0:T(1024)(128)(4,1)} %bitcast.162), calls=%async_computation.28 | async-start | bytes 8388608
  1500.6 30.2 %slice-start.9 = ((s8[18874368]{0:T(1024)(128)(4,1)}), s8[4194304]{0:T(1024)(128)(4,1)S(1)}, s32[]{:S(2)}) async-start(s8[18874368]{0:T(1024)(128)(4,1)} %bitcast.162), calls=%async_computation.29 | async-start | bytes 8388608
  1513.9 16.9 slice-start.10
  1513.9 16.9 slice-start.11
Sparse Core Ops, SparseCore 0:
  11.0 66.3 all-gather.12
  80.4 61.9 all-gather.10
  146.5 45.1 all-gather.14
  194.6 80.3 all-gather.16
  277.8 80.0 all-gather.18
  360.8 235.5 all-gather.22
  599.4 235.1 all-gather.20
  837.6 235.1 all-gather.24
  1200.0 48.0 reduce-scatter.15
  1251.0 122.4 all-gather.28
  1376.6 123.9 all-gather.26
  1506.9 134.4 reduce-scatter.9
  1647.9 135.1 reduce-scatter.11
  1789.9 205.7 reduce-scatter.7
  2002.5 206.0 reduce-scatter.13
where the time goes:
time: 2220 us
  waiting for transfers between devices  1760 us (79%)
  matrix products  294 us (13%)
  blocking collectives  84.6 us (4%)
  local copies, waits for them, and re-layouts  42 us (2%)
    all_gather x1, waiting for transfers between devices, on_device(): up_piece = lax.all_gather(up_weight, ('batch', 'ctx'), axis=0, tiled=True)  231 us
    all_gather x1, waiting for transfers between devices, on_device(): lax.all_gather(gate_weight, ('batch', 'ctx'), axis=0, tiled=True)  216 us
    all_gather x1, waiting for transfers between devices, on_device(): lax.all_gather(down_weight, ('batch', 'ctx'), axis=0, tiled=True)  216 us
    reduce_scatter x1, waiting for transfers between devices, on_device(): lax.psum_scatter(out_term, ('batch', 'ctx'), scatter_dimension=0, tiled=T...  213 us
    reduce_scatter x1, waiting for transfers between devices, on_device(): lax.psum_scatter(query_term, ('batch', 'ctx'), scatter_dimension=0, tiled...  213 us
    reduce_scatter x1, waiting for transfers between devices, on_device(): lax.psum_scatter(value_term, ('batch', 'ctx'), scatter_dimension=0, tiled...  142 us
    dot_general x10, matrix products, rows_product(): lax.dot_general(left_mat, right_mat, (((1,), (1,)), ((), ())), preferred_...  118 us
    all_gather x1, waiting for transfers between devices, on_device(): lax.all_gather(normed_mid, ('batch', 'ctx'), axis=0, tiled=True)  93.9 us
  transfers between devices with their start and end apart: 15, of which 15 were waited for; matrix products, arithmetic and copies ran while one was open for 10% of the time, Pallas kernels for 0%

commit v1 on v0

v1 whole, which is shorter than its diff:
```python
import functools
import math

import jax
import jax.numpy as jnp
from jax import lax
from jax.sharding import PartitionSpec as P


HEADS = 8
KV_HEADS = 4
HEAD_DIM = 256

NORM_EPS = 1e-06
SOFT_CAP = 50.0

BF16 = jnp.bfloat16
F32 = jnp.float32


def normalize(values_in, gain_vec):
    inv_rms = lax.rsqrt(jnp.mean(values_in * values_in, axis=-1, keepdims=True) + NORM_EPS)
    return (values_in * inv_rms * gain_vec.astype(F32), inv_rms)


def norm_back(values_in, inv_rms, gain_vec, grad_in):
    scaled = values_in * inv_rms
    weighted = grad_in * gain_vec.astype(F32)
    grad_gain = jnp.sum(grad_in * scaled, axis=0)
    grad_values = inv_rms * (
        weighted - scaled * jnp.mean(weighted * scaled, axis=-1, keepdims=True)
    )
    return (grad_values, grad_gain)


def geglu(gate_val, up_val):
    return jax.nn.gelu(gate_val, approximate=True) * up_val


def product(left_mat, right_mat):
    return jnp.dot(left_mat, right_mat, preferred_element_type=F32)


def rows_product(left_mat, right_mat):
    return lax.dot_general(
        left_mat, right_mat, (((1,), (1,)), ((), ())), preferred_element_type=F32
    )


def cols_product(left_mat, right_mat):
    return lax.dot_general(
        left_mat, right_mat, (((0,), (0,)), ((), ())), preferred_element_type=F32
    )


class Line:
    def __init__(self, ctx_size):
        self.size = ctx_size // 2
        self.index = lax.axis_index("ctx")
        self.at = self.index // 2
        self.parity = self.index % 2
        self.sources = []
        for z in range(self.size):
            first = 1 if z < self.size / 2 else -1
            reach = [d for k in range(1, self.size) for d in (k * first, -k * first)]
            self.sources.append([0] + [d for d in reach if 0 <= z + d < self.size])

    def move(self, rows, step, froms):
        pairs = [(2 * z + p, 2 * (z + step) + p) for z in froms for p in range(2)]
        return lax.ppermute(rows, "ctx", pairs)

    def partner(self, rows):
        return lax.ppermute(rows, "ctx", [(c, c ^ 1) for c in range(2 * self.size)])

    def pick(self, options):
        known = [o for o in options if o is not None]
        result = known[0]
        for other in {id(o): o for o in known[1:] if o is not known[0]}.values():
            places = [z for z, o in enumerate(options) if o is other]
            here = self.at == places[0]
            for z in places[1:]:
                here = here | (self.at == z)
            result = jnp.where(here, other, result)
        return result

    def gather(self, rows, work=None):
        arrived, slots, results = {0: rows}, [rows], []
        for k in range(1, self.size):
            arrived[-k] = self.move(arrived[1 - k], 1, range(k - 1, self.size - 1))
            arrived[k] = self.move(arrived[k - 1], -1, range(1, self.size - k + 1))
            if work is not None:
                results.append(work(k, slots))
            slots.append(
                self.pick([arrived[self.sources[z][k]] for z in range(self.size)])
            )
        return slots, results

    def part_for(self, parts, distance):
        return self.pick(
            [
                parts[self.sources[z].index(distance)] if distance in self.sources[z] else None
                for z in range(self.size)
            ]
        )

    def scatter(self, parts, work=()):
        upward = downward = 0.0
        results = []
        for step, k in enumerate(range(self.size - 1, 0, -1), 1):
            upward = (self.part_for(parts, k) + upward).astype(BF16)
            downward = (self.part_for(parts, -k) + downward).astype(BF16)
            if step <= len(work):
                function, given = work[step - 1]
                upward, downward, given = lax.optimization_barrier((upward, downward, given))
            upward = self.move(upward, 1, range(self.size - k)).astype(F32)
            downward = self.move(downward, -1, range(k, self.size)).astype(F32)
            if step <= len(work):
                results.append(function(*given))
        return parts[0] + upward + downward, results

    def shift(self, rows, k):
        pairs = [
            (2 * ((z + k) % self.size) + p, 2 * z + p) for z in range(self.size) for p in range(2)
        ]
        return lax.ppermute(rows, "ctx", pairs)

    def slot_blocks(self, block_row, parity):
        table = [[z + d for d in self.sources[z]] for z in range(self.size)]
        positions = lax.dynamic_index_in_dim(
            jnp.asarray(table, jnp.int32), self.at, axis=0, keepdims=False
        )
        ids = jnp.arange(block_row.shape[0], dtype=jnp.int32)
        matches = ids[None, :] == (2 * positions + parity)[:, None]
        return jnp.sum(jnp.where(matches, block_row[None, :], 0), axis=1)


def across(rows, bit, batch_size):
    return lax.ppermute(rows, "batch", [(b, b ^ bit) for b in range(batch_size)])


def cube_order(bits):
    order = [0]
    for bit in bits:
        order = order + [mask ^ bit for mask in order]
    return order


def cube_gather(rows, bits, batch_size):
    pieces = [rows]
    for bit in bits:
        more = []
        for piece in pieces:
            more.append(across(piece, bit, batch_size))
        pieces = pieces + more
    return [pieces[cube_order(bits).index(k)] for k in range(batch_size)]


def batch_scatter(pieces, batch_index, batch_size):
    def piece(k):
        return lax.dynamic_index_in_dim(pieces, batch_index ^ k, axis=0, keepdims=False)

    total = piece(0).astype(F32)
    received = [across(piece(k), k, batch_size) for k in range(1, batch_size)]
    return sum((one.astype(F32) for one in received), total)


def cube_send(pieces, bit, batch_size):
    half = len(pieces) // 2
    return [across(piece.astype(BF16), bit, batch_size) for piece in pieces[half:]]


def cube_add(pieces, sent):
    half = len(pieces) // 2
    return [own.astype(F32) + other.astype(F32) for own, other in zip(pieces[:half], sent)]


def everywhere(array, line, batch_size):
    array = sum((line.shift(array, k) for k in range(1, line.size)), array)
    array = sum((across(array, k, batch_size) for k in range(1, batch_size)), array)
    return array + line.partner(array)


def on_device(
    sizes,
    inputs,
    block_order,
    cotangent,
    attn_gain,
    post_attn_gain,
    ffn_gain,
    post_ffn_gain,
    query_weight,
    key_weight,
    value_weight,
    out_weight,
    gate_weight,
    up_weight,
    down_weight,
):
    batch_size, ctx_size = sizes
    line = Line(ctx_size)
    devices = batch_size * ctx_size
    flat_index = lax.axis_index("batch") * ctx_size + line.index
    local_rows = inputs.shape[1]
    features = inputs.shape[2]
    rows_x = inputs.reshape(local_rows, features)
    grad_y = cotangent.reshape(local_rows, features)
    block_row = block_order.reshape(-1)
    scale = 1.0 / math.sqrt(HEAD_DIM)
    line_rows = local_rows * line.size
    heads = HEADS // line.size
    sharing = line.size // KV_HEADS
    query_width = heads * HEAD_DIM
    bits_up = [1 << i for i in range(batch_size.bit_length() - 1)]
    bits_down = bits_up[::-1]
    owner_pairs = [
        (c * batch_size + b, b * ctx_size + c) for b in range(batch_size) for c in range(ctx_size)
    ]

    def slots(rows):
        return [
            rows[slot * local_rows : (slot + 1) * local_rows] for slot in range(line.size)
        ]

    def stack(parts):
        return jnp.concatenate(parts, axis=0)

    own_gains = jnp.stack((attn_gain, post_attn_gain, ffn_gain, post_ffn_gain))
    piece = own_gains.shape[1]
    spread = lax.dynamic_update_slice(
        jnp.zeros((4, devices, piece), BF16), own_gains[:, None], (0, flat_index, 0)
    )
    gains = everywhere(spread, line, batch_size).reshape(4, features)
    gain_one, gain_two, gain_three, gain_four = gains[0], gains[1], gains[2], gains[3]

    weight_rows = query_weight.shape[0]

    def kv_targets(weight):
        return jnp.repeat(weight.reshape(weight_rows, KV_HEADS, HEAD_DIM), sharing, axis=1)

    def from_here(stacked):
        return lax.dynamic_slice_in_dim(
            jnp.concatenate((stacked, stacked), axis=0), line.at, line.size, axis=0
        )

    def from_start(turned):
        return lax.dynamic_slice_in_dim(
            jnp.concatenate((turned, turned), axis=0),
            (line.size - line.at) % line.size,
            line.size,
            axis=0,
        )

    per_target = jnp.concatenate(
        (
            query_weight.reshape(weight_rows, line.size, query_width),
            kv_targets(key_weight),
            kv_targets(value_weight),
        ),
        axis=2,
    )
    turned = from_here(jnp.transpose(per_target, (1, 0, 2)))
    received = [turned[0]] + [
        line.shift(turned[line.size - k], k) for k in range(1, line.size)
    ]
    batch_index = lax.axis_index("batch")
    even = line.parity == 0

    def placed(pieces, shape, block):
        whole = jnp.zeros(shape, BF16)
        for k, one in enumerate(pieces):
            for parity, rows in ((line.parity, one), (1 - line.parity, line.partner(one))):
                start, update = block(batch_index ^ k, parity, rows)
                whole = lax.dynamic_update_slice(whole, update, start)
        return whole

    w_half = from_start(jnp.stack(received))
    pieces = cube_gather(w_half, bits_up, batch_size)
    w_qkv = placed(
        pieces,
        (batch_size, line.size, 2) + w_half.shape[1:],
        lambda b, parity, rows: ((b, 0, parity, 0, 0), rows[None, :, None]),
    ).reshape(features, query_width + 2 * HEAD_DIM)

    out_half = lax.ppermute(out_weight, ("batch", "ctx"), owner_pairs)
    out_pieces = cube_gather(out_half, bits_up, batch_size)
    w_out = placed(
        out_pieces,
        (2, batch_size) + out_half.shape,
        lambda b, parity, rows: ((parity, b, 0, 0), rows[None, None]),
    ).reshape(-1, features)

    unit_rows = gate_weight.shape[0]
    gate_pieces = cube_gather(gate_weight, bits_up, batch_size)
    up_pieces = cube_gather(up_weight, bits_down, batch_size)
    down_pieces = cube_gather(down_weight, bits_up, batch_size)

    normed, inv_one = normalize(rows_x, gain_one)
    normed_in, _ = line.gather(normed.astype(BF16))
    qkv = stack([product(rows, w_qkv).astype(BF16) for rows in normed_in])
    own_kv = qkv[:, query_width:]
    kv = stack((own_kv, line.partner(own_kv)))
    keys = kv[:, :HEAD_DIM]
    values = kv[:, HEAD_DIM:]

    def by_head(rows):
        return stack([rows[:, h * HEAD_DIM : (h + 1) * HEAD_DIM] for h in range(heads)])

    def by_row(stacked):
        return jnp.concatenate(
            [stacked[h * line_rows : (h + 1) * line_rows] for h in range(heads)], axis=1
        )

    query = by_head(qkv[:, :query_width])

    def row_positions(blocks):
        inside = jnp.arange(local_rows, dtype=jnp.int32)
        return (blocks[:, None] * local_rows + inside[None, :]).reshape(-1)

    query_pos = row_positions(line.slot_blocks(block_row, line.parity))
    key_pos = jnp.concatenate(
        (query_pos, row_positions(line.slot_blocks(block_row, 1 - line.parity)))
    )
    visible = key_pos[None, :] <= jnp.tile(query_pos, heads)[:, None]
    tanh_val = jnp.tanh(rows_product(query, keys) * scale / SOFT_CAP)
    raw = jnp.where(visible, jnp.exp(SOFT_CAP * tanh_val), 0.0)
    totals = jnp.sum(raw, axis=1, keepdims=True)
    attended = (product(raw.astype(BF16), values) / totals).astype(BF16)
    attended_rows = by_row(attended)
    branch, _ = line.scatter(slots(product(attended_rows, w_out)))
    branch_normed, inv_two = normalize(branch, gain_two)
    middle = rows_x + branch_normed
    normed_m, inv_three = normalize(middle, gain_three)

    def with_partner(rows):
        return stack((rows, line.partner(rows)))

    def pair_sum(part):
        other = line.partner(part[local_rows:].astype(BF16))
        return part[:local_rows] + other.astype(F32)

    def expand(rows):
        both = with_partner(rows)
        gate_act = rows_product(both, w_gate)
        up_act = rows_product(both, w_up)
        return both, gate_act, up_act, geglu(gate_act, up_act).astype(BF16)

    def contract(forward):
        return pair_sum(product(forward[3], w_down))

    expanded, parts = [], []

    w_gate, w_up = stack(gate_pieces), stack(up_pieces)
    w_down = stack(down_pieces)

    def forward_work(k, arrived):
        expanded.append(expand(arrived[k - 1]))
        if k > 1:
            parts.append(contract(expanded[k - 2]))

    normed_rows, _ = line.gather(normed_m.astype(BF16), forward_work)
    expanded.append(expand(normed_rows[-1]))
    last = contract(expanded[-1])
    parts = parts + [contract(expanded[-2]), last]
    mid_rows = stack([e[0] for e in expanded])
    ffn_out, _ = line.scatter(parts)
    ffn_normed, inv_four = normalize(ffn_out, gain_four)
    output = middle + ffn_normed

    grad_ffn, grad_four = norm_back(ffn_out, inv_four, gain_four, grad_y)

    def shrink(rows, forward):
        both = with_partner(rows)
        _, pull_back = jax.vjp(geglu, forward[1], forward[2])
        gate_part, up_part = pull_back(rows_product(both, w_down))
        gate_part, up_part = gate_part.astype(BF16), up_part.astype(BF16)
        part = product(gate_part, w_gate) + product(up_part, w_up)
        return both, gate_part, up_part, pair_sum(part)

    ffn_rows, results = line.gather(
        grad_ffn.astype(BF16), lambda k, arrived: shrink(arrived[k - 1], expanded[k - 1])
    )
    shrunk = list(results) + [shrink(ffn_rows[-1], expanded[-1])]
    ffn_rows = stack([e[0] for e in shrunk])
    hidden = stack([e[3] for e in expanded])
    grad_gate = stack([e[1] for e in shrunk])
    grad_up = stack([e[2] for e in shrunk])

    def unit_grads(left, right, bits):
        total = cols_product(left, right).astype(BF16)
        pieces = [total[i * unit_rows : (i + 1) * unit_rows] for i in cube_order(bits)]
        return pieces, cube_send(pieces, bits[-1], batch_size)

    def first_sum(pieces, sent, bits):
        pieces = cube_add(pieces, sent)
        if len(bits) == 1:
            return pieces, None
        return pieces, cube_send(pieces, bits[-2], batch_size)

    def rest(pieces, sent, bits):
        for bit in reversed(bits[:-1]):
            sent = cube_send(pieces, bit, batch_size) if sent is None else sent
            pieces, sent = cube_add(pieces, sent), None
        return pieces[0]

    grad_nm, (down_sum, gate_sum, up_sum) = line.scatter(
        [e[3] for e in shrunk],
        (
            (functools.partial(unit_grads, bits=bits_up), (hidden, ffn_rows)),
            (functools.partial(unit_grads, bits=bits_down), (grad_gate, mid_rows)),
            (functools.partial(unit_grads, bits=bits_up), (grad_up, mid_rows)),
        ),
    )

    grad_mid_part, grad_three = norm_back(middle, inv_three, gain_three, grad_nm)
    grad_mid = grad_y + grad_mid_part
    grad_branch, grad_two = norm_back(branch, inv_two, gain_two, grad_mid)
    gain_grads = jnp.stack((grad_two, grad_three, grad_four))

    gain_grads = everywhere(gain_grads, line, batch_size)
    gain_grads = lax.dynamic_slice_in_dim(gain_grads, flat_index * piece, piece, axis=1)

    def back_work(k, arrived):
        if k == line.size - 2:
            return first_sum(*down_sum, bits_up)
        if k == line.size - 1:
            return first_sum(*gate_sum, bits_down)

    branch_rows, back_results = line.gather(grad_branch.astype(BF16), back_work)
    grad_branch_b = stack(branch_rows)
    down_grad = rest(*back_results[-2], bits_up)
    gate_grad = rest(*back_results[-1], bits_down)
    grad_att = by_head(rows_product(grad_branch_b, w_out).astype(BF16))
    delta = jnp.sum(grad_att.astype(F32) * attended.astype(F32), axis=1, keepdims=True)
    prob = raw / totals
    dprob = rows_product(grad_att, values)
    grad_z = (prob * (dprob - delta) * (1.0 - tanh_val * tanh_val) * scale).astype(BF16)
    grad_query = by_row(product(grad_z, keys).astype(BF16))
    grad_kv = jnp.concatenate(
        (cols_product(grad_z, query), cols_product(prob.astype(BF16), grad_att)), axis=1
    )
    grad_kv = grad_kv[:line_rows] + line.partner(grad_kv[line_rows:])
    grad_qkv = jnp.concatenate((grad_query, grad_kv.astype(BF16)), axis=1)

    def qkv_work(rows, grads):
        part = cols_product(rows, grads).astype(BF16).reshape(
            batch_size, line.size, 2, weight_rows, -1
        )
        part_even, part_odd = part[:, :, 0], part[:, :, 1]
        other = line.partner(jnp.where(even, part_odd, part_even))
        return jnp.where(even, part_even, part_odd), other

    grad_in, (qkv_parts, up_sum) = line.scatter(
        slots(rows_product(grad_qkv, w_qkv)),
        (
            (qkv_work, (stack(normed_in), grad_qkv)),
            (lambda: first_sum(*up_sum, bits_up), ()),
        ),
    )
    up_grad = rest(*up_sum, bits_up)
    qkv_part = (qkv_parts[0].astype(F32) + qkv_parts[1].astype(F32)).astype(BF16)

    out_part = cols_product(attended_rows, grad_branch_b).reshape(2, -1, features)
    out_other = line.partner(jnp.where(even, out_part[1], out_part[0]).astype(BF16))
    out_part = jnp.where(even, out_part[0], out_part[1]) + out_other.astype(F32)
    out_part = batch_scatter(
        out_part.astype(BF16).reshape(batch_size, -1, features), batch_index, batch_size
    )
    out_grad = lax.ppermute(
        out_part.astype(BF16), ("batch", "ctx"), [(there, here) for here, there in owner_pairs]
    ).astype(F32)

    qkv_part = batch_scatter(qkv_part, batch_index, batch_size)
    turned = from_here(qkv_part.astype(BF16))
    returned = [turned[0]] + [
        line.shift(turned[line.size - k], k) for k in range(1, line.size)
    ]
    returned = from_start(jnp.stack(returned)).astype(F32)

    def columns(part):
        return jnp.transpose(part, (1, 0, 2)).reshape(weight_rows, -1)

    def kv_columns(part):
        part = part.reshape(KV_HEADS, sharing, weight_rows, HEAD_DIM)
        return columns(jnp.sum(part, axis=1))

    query_grad = columns(returned[:, :, :query_width])
    key_grad = kv_columns(returned[:, :, query_width : query_width + HEAD_DIM])
    value_grad = kv_columns(returned[:, :, query_width + HEAD_DIM :])

    grad_x_part, _ = norm_back(rows_x, inv_one, gain_one, grad_in)
    input_grad = grad_mid + grad_x_part
    attn_gain_grad = (
        jnp.sum(query_weight.astype(F32) * query_grad, axis=1)
        + jnp.sum(key_weight.astype(F32) * key_grad, axis=1)
        + jnp.sum(value_weight.astype(F32) * value_grad, axis=1)
    ) / attn_gain.astype(F32)
    return (
        output.reshape(1, local_rows, features),
        input_grad.reshape(1, local_rows, features),
        query_grad,
        key_grad,
        value_grad,
        out_grad,
        gate_grad,
        up_grad,
        down_grad,
        attn_gain_grad,
        gain_grads[0],
        gain_grads[1],
        gain_grads[2],
    )


def solution(mesh):
    sizes = (mesh.shape["batch"], mesh.shape["ctx"])
    rows = P("batch", "ctx", None)
    owned = P(("batch", "ctx"), None)
    vector = P(("batch", "ctx"))

    def program(*args):
        return on_device(sizes, *args)

    return jax.shard_map(
        program,
        mesh=mesh,
        in_specs=(rows, P("batch", None), rows) + (vector,) * 4 + (owned,) * 7,
        out_specs=(rows, rows) + (owned,) * 7 + (vector,) * 4,
        check_vma=False,
    )
```

time: 2220 us -> 752 us (0.34)
  waiting for transfers between devices: 1760 us -> 352 us
  matrix products: 294 us -> 99.4 us
  starting transfers between devices: 0.8 us -> 192 us
  blocking collectives: 84.6 us -> 0 us
  other arithmetic: 20.7 us -> 47.2 us
    all_gather x10 -> x0, waiting for transfers between devices: 1060 us -> none  [the longest x1 231 us: on_device(): up_piece = lax.all_gather(up_weight, ('batch', 'ctx'), axis=0, tiled=True)]
    reduce_scatter x4 -> x0, waiting for transfers between devices: 646 us -> none  [the longest x1 213 us: on_device(): lax.psum_scatter(out_term, ('batch', 'ctx'), scatter_dimension=0, tiled=T...]
    ppermute x0 -> x128, waiting for transfers between devices: none -> 352 us  [the longest x36 174 us: across(): lax.ppermute(rows, 'batch', [(b, b ^ bit) for b in range(batch_size)])]
    ppermute x0 -> x128, starting transfers between devices: none -> 192 us  [the longest x48 120 us: move(): return lax.ppermute(rows, 'ctx', pairs)]
    unnamed x2 -> x0, blocking collectives: 84.6 us -> none
    dot_general x10 -> x16, matrix products: 118 us -> 37.3 us  [rows_product(): lax.dot_general(left_mat, right_mat, (((1,), (1,)), ((), ())), preferred_...]
    dot_general x13 -> x19, matrix products: 99.8 us -> 29.9 us  [product(): return jnp.dot(left_mat, right_mat, preferred_element_type=F32)]
    unnamed x16 -> x0, waiting for transfers between devices: 52.6 us -> none
  transfers between devices with their start and end apart: 15 -> 128, of which waited for: 15 -> 55; matrix products, arithmetic and copies ran while one was open for 10% -> 23% of each run, Pallas kernels for 0% -> 0%
where the time goes in v1:
time: 752 us; the launch traced here: 743 us
  waiting for transfers between devices  352 us (47%)
  starting transfers between devices  192 us (26%)
  matrix products  99.4 us (13%)
  local copies, waits for them, and re-layouts  48.1 us (6%)
  other arithmetic  47.2 us (6%)
    ppermute x36, waiting for transfers between devices, across(): lax.ppermute(rows, 'batch', [(b, b ^ bit) for b in range(batch_size)])  174 us
    ppermute x48, waiting for transfers between devices, move(): return lax.ppermute(rows, 'ctx', pairs)  150 us
    ppermute x48, starting transfers between devices, move(): return lax.ppermute(rows, 'ctx', pairs)  120 us
    ppermute x36, starting transfers between devices, across(): lax.ppermute(rows, 'batch', [(b, b ^ bit) for b in range(batch_size)])  43.5 us
    dot_general x16, matrix products, rows_product(): lax.dot_general(left_mat, right_mat, (((1,), (1,)), ((), ())), preferred_...  37.3 us
    dot_general x7, matrix products, cols_product(): lax.dot_general(left_mat, right_mat, (((0,), (0,)), ((), ())), preferred_...  32.2 us
    dot_general x19, matrix products, product(): return jnp.dot(left_mat, right_mat, preferred_element_type=F32)  29.9 us
    unnamed x244, local copies, waits for them, and re-layouts  25.6 us
  transfers between devices with their start and end apart: 128, of which 55 were waited for; matrix products, arithmetic and copies ran while one was open for 23% of the time, Pallas kernels for 0%

profile of v1, /device:TPU:0, one launch (start us, length us, event | category | flops | bytes accessed | tf_op | source)
XLA Modules:
  0.0 742.6 jit_solution(6694328769816098093)
XLA Ops:
  1.4 3.1 collective-permute-start.2
  8.4 3.8 collective-permute-start.24
  31.4 10.6 %collective-permute-done.7 = bf16[72,1024]{1,0:T(8,128)(2,1)S(1)} collective-permute-done((bf16[72,1024]{1,0:T(8,128)(2,1)S(1)}, bf16[72,1024]{1,0:T(8,128)(2,1)S(1)}, u32[]{:S(2)}, u32[]{:S(2)}) %collective-permute-start.7) | collective-permute-done | bytes 147488 | tf_op jit(solution)/shard_map/ppermute | solution.py:125
  45.0 3.6 concatenate.100
  54.1 16.8 %collective-permute-done.26 = bf16[64,2304]{1,0:T(8,128)(2,1)S(1)} collective-permute-done((bf16[64,2304]{1,0:T(8,128)(2,1)}, bf16[64,2304]{1,0:T(8,128)(2,1)S(1)}, u32[]{:S(2)}, u32[]{:S(2)}) %collective-permute-start.26) | collective-permute-done | bytes 294944 | tf_op jit(solution)/shard_map/ppermute | solution.py:138
  73.6 7.4 %collective-permute-done.28 = bf16[64,2304]{1,0:T(8,128)(2,1)S(1)} collective-permute-done((bf16[64,2304]{1,0:T(8,128)(2,1)}, bf16[64,2304]{1,0:T(8,128)(2,1)S(1)}, u32[]{:S(2)}, u32[]{:S(2)}) %collective-permute-start.28) | collective-permute-done | bytes 294944 | tf_op jit(solution)/shard_map/ppermute | solution.py:138
  85.3 8.4 %collective-permute-done.13 = bf16[4,72,1024]{2,0,1:T(4,128)(2,1)S(1)} collective-permute-done((bf16[4,72,1024]{2,0,1:T(4,128)(2,1)S(1)}, bf16[4,72,1024]{2,0,1:T(4,128)(2,1)S(1)}, u32[]{:S(2)}, u32[]{:S(2)}) %collective-permute-start.13) | collective-permute-done | bytes 589856 | tf_op jit(solution)/shard_map/ppermute | solution.py:138
  93.7 6.3 collective-permute-done.30
  103.3 7.7 %collective-permute-done.15 = bf16[4,72,1024]{2,0,1:T(4,128)(2,1)S(1)} collective-permute-done((bf16[4,72,1024]{2,0,1:T(4,128)(2,1)S(1)}, bf16[4,72,1024]{2,0,1:T(4,128)(2,1)S(1)}, u32[]{:S(2)}, u32[]{:S(2)}) %collective-permute-start.15) | collective-permute-done | bytes 589856 | tf_op jit(solution)/shard_map/ppermute | solution.py:138
  111.4 6.4 collective-permute-done.22
  137.7 6.9 collective-permute-done.32
  144.8 4.6 collective-permute-start.33
  155.3 6.2 collective-permute-done.33
  170.8 13.4 %collective-permute-start.34 = (bf16[128,2304]{1,0:T(8,128)(2,1)S(1)}, bf16[128,2304]{1,0:T(8,128)(2,1)S(1)}, u32[]{:S(2)}, u32[]{:S(2)}) collective-permute-start(bf16[128,2304]{1,0:T(8,128)(2,1)S(1)} %get-tuple-element.103), channel_id=1, source_target_pairs={{0,2},{1,3},{2,4},{3,5},{4,6},{5,7},{8,10},{9,11},{10,12},{11,13},... | collective-permute-start | bytes 1769480 | tf_op jit(solution)/shard_map/ppermute | solution.py:70
  184.4 8.0 %collective-permute-done.42 = bf16[288,2304]{1,0:T(8,128)(2,1)} collective-permute-done((bf16[288,2304]{1,0:T(8,128)(2,1)}, bf16[288,2304]{1,0:T(8,128)(2,1)}, u32[]{:S(2)}, u32[]{:S(2)}) %collective-permute-start.42) | collective-permute-done | bytes 1327136 | tf_op jit(solution)/shard_map/ppermute | solution.py:138
  198.6 9.1 %collective-permute-done.37 = bf16[128,2304]{1,0:T(8,128)(2,1)S(1)} collective-permute-done((bf16[128,2304]{1,0:T(8,128)(2,1)S(1)}, bf16[128,2304]{1,0:T(8,128)(2,1)S(1)}, u32[]{:S(2)}, u32[]{:S(2)}) %collective-permute-start.37) | collective-permute-done | bytes 589856 | tf_op jit(solution)/shard_map/ppermute | solution.py:70
  208.8 12.0 %collective-permute-done.45 = bf16[288,2304]{1,0:T(8,128)(2,1)S(1)} collective-permute-done((bf16[288,2304]{1,0:T(8,128)(2,1)}, bf16[288,2304]{1,0:T(8,128)(2,1)S(1)}, u32[]{:S(2)}, u32[]{:S(2)}) %collective-permute-start.45) | collective-permute-done | bytes 1327136 | tf_op jit(solution)/shard_map/ppermute | solution.py:138
  222.4 4.6 collective-permute-start.49
  227.9 8.4 %collective-permute-done.51 = bf16[128,2304]{1,0:T(8,128)(2,1)S(1)} collective-permute-done((bf16[128,2304]{1,0:T(8,128)(2,1)S(1)}, bf16[128,2304]{1,0:T(8,128)(2,1)S(1)}, u32[]{:S(2)}, u32[]{:S(2)}) %collective-permute-start.51) | collective-permute-done | bytes 589856 | tf_op jit(solution)/shard_map/ppermute | solution.py:70
  237.7 11.8 %collective-permute-done.41 = bf16[288,2304]{1,0:T(8,128)(2,1)S(1)} collective-permute-done((bf16[288,2304]{1,0:T(8,128)(2,1)}, bf16[288,2304]{1,0:T(8,128)(2,1)S(1)}, u32[]{:S(2)}, u32[]{:S(2)}) %collective-permute-start.41) | collective-permute-done | bytes 1327136 | tf_op jit(solution)/shard_map/ppermute | solution.py:138
  251.8 12.6 %collective-permute-done.52 = bf16[128,2304]{1,0:T(8,128)(2,1)S(1)} collective-permute-done((bf16[128,2304]{1,0:T(8,128)(2,1)S(1)}, bf16[128,2304]{1,0:T(8,128)(2,1)S(1)}, u32[]{:S(2)}, u32[]{:S(2)}) %collective-permute-start.52) | collective-permute-done | bytes 589856 | tf_op jit(solution)/shard_map/ppermute | solution.py:70
  264.9 11.9 %collective-permute-done.47 = bf16[288,2304]{1,0:T(8,128)(2,1)S(1)} collective-permute-done((bf16[288,2304]{1,0:T(8,128)(2,1)S(1)}, bf16[288,2304]{1,0:T(8,128)(2,1)S(1)}, u32[]{:S(2)}, u32[]{:S(2)}) %collective-permute-start.47) | collective-permute-done | bytes 1327136 | tf_op jit(solution)/shard_map/ppermute | solution.py:138
  281.1 11.8 %collective-permute-done.58 = bf16[128,2304]{1,0:T(8,128)(2,1)S(1)} collective-permute-done((bf16[128,2304]{1,0:T(8,128)(2,1)S(1)}, bf16[128,2304]{1,0:T(8,128)(2,1)S(1)}, u32[]{:S(2)}, u32[]{:S(2)}) %collective-permute-start.58) | collective-permute-done | bytes 589856 | tf_op jit(solution)/shard_map/ppermute | solution.py:70
  315.7 8.2 %collective-permute-done.61 = bf16[128,2304]{1,0:T(8,128)(2,1)S(1)} collective-permute-done((bf16[128,2304]{1,0:T(8,128)(2,1)S(1)}, bf16[128,2304]{1,0:T(8,128)(2,1)S(1)}, u32[]{:S(2)}, u32[]{:S(2)}) %collective-permute-start.61) | collective-permute-done | bytes 589856 | tf_op jit(solution)/shard_map/ppermute | solution.py:70
  324.3 4.4 collective-permute-start.62
  336.3 4.6 collective-permute-done.62
  342.4 7.2 collective-permute-start.63
  355.2 5.1 collective-permute-done.63
  360.3 5.0 collective-permute-done.66
  372.2 4.8 collective-permute-start.69
  378.8 9.1 %collective-permute-done.71 = bf16[128,2304]{1,0:T(8,128)(2,1)S(1)} collective-permute-done((bf16[128,2304]{1,0:T(8,128)(2,1)S(1)}, bf16[128,2304]{1,0:T(8,128)(2,1)S(1)}, u32[]{:S(2)}, u32[]{:S(2)}) %collective-permute-start.71) | collective-permute-done | bytes 589856 | tf_op jit(solution)/shard_map/ppermute | solution.py:70
  400.4 12.0 %collective-permute-done.72 = bf16[128,2304]{1,0:T(8,128)(2,1)S(1)} collective-permute-done((bf16[128,2304]{1,0:T(8,128)(2,1)S(1)}, bf16[128,2304]{1,0:T(8,128)(2,1)S(1)}, u32[]{:S(2)}, u32[]{:S(2)}) %collective-permute-start.72) | collective-permute-done | bytes 589856 | tf_op jit(solution)/shard_map/ppermute | solution.py:70
  423.1 12.6 %collective-permute-done.78 = bf16[128,2304]{1,0:T(8,128)(2,1)S(1)} collective-permute-done((bf16[128,2304]{1,0:T(8,128)(2,1)S(1)}, bf16[128,2304]{1,0:T(8,128)(2,1)S(1)}, u32[]{:S(2)}, u32[]{:S(2)}) %collective-permute-start.78) | collective-permute-done | bytes 589856 | tf_op jit(solution)/shard_map/ppermute | solution.py:70
  436.8 3.9 fusion.26
  447.2 4.4 fusion.145
  458.0 8.5 %convolution_convert_fusion = bf16[1152,2304]{1,0:T(8,128)(2,1)S(1)} fusion(bf16[1024,1152]{1,0:T(8,128)(2,1)S(1)} %pad_maximum_fusion, bf16[1024,2304]{1,0:T(8,128)(2,1)} %constant_dynamic-update-slice_fusion.12), kind=kOutput, calls=%fused_computation | convolution fusion | flops 5438472192 | bytes 12386304 | tf_op jit(solution)/shard_map/dot_general | solution.py:51
  470.5 4.4 collective-permute-start.83
  475.6 8.5 %convolution_convert_fusion.2 = bf16[1152,2304]{1,0:T(8,128)(2,1)S(1)} fusion(bf16[1024,1152]{1,0:T(8,128)(2,1)S(1)} %pad_maximum_fusion.1, bf16[1024,2304]{1,0:T(8,128)(2,1)} %constant_dynamic-update-slice_fusion.20), kind=kOutput, calls=%fused_computation.2 | convolution fusion | flops 5438472192 | bytes 12386304 | tf_op jit(solution)/shard_map/dot_general | solution.py:51
  488.3 10.6 %collective-permute-start.85 = (bf16[128,2304]{1,0:T(8,128)(2,1)}, bf16[128,2304]{1,0:T(8,128)(2,1)S(1)}, u32[]{:S(2)}, u32[]{:S(2)}) collective-permute-start(bf16[128,2304]{1,0:T(8,128)(2,1)} %get-tuple-element.35), channel_id=1, source_target_pairs={{0,2},{1,3},{2,4},{3,5},{4,6},{5,7},{8,10},{9,11},{10,12},{11,13},... | collective-permute-start | bytes 1769480 | tf_op jit(solution)/shard_map/ppermute | solution.py:70
  500.2 8.5 %convolution_convert_fusion.1 = bf16[1152,2304]{1,0:T(8,128)(2,1)S(1)} fusion(bf16[1024,1152]{1,0:T(8,128)(2,1)S(1)} %pad_maximum_fusion.2, bf16[1024,2304]{1,0:T(8,128)(2,1)} %constant_dynamic-update-slice_fusion.20), kind=kOutput, calls=%fused_computation.1 | convolution fusion | flops 5438472192 | bytes 12386304 | tf_op jit(solution)/shard_map/dot_general | solution.py:51
  516.9 9.3 %collective-permute-done.119 = bf16[288,2304]{1,0:T(8,128)(2,1)S(1)} collective-permute-done((bf16[288,2304]{1,0:T(8,128)(2,1)S(1)}, bf16[288,2304]{1,0:T(8,128)(2,1)S(1)}, u32[]{:S(2)}, u32[]{:S(2)}) %collective-permute-start.119) | collective-permute-done | bytes 1327136 | tf_op jit(solution)/shard_map/ppermute | solution.py:138
  526.2 4.7 collective-permute-start.121
  536.1 4.6 collective-permute-done.126
  546.5 26.3 %collective-permute-done.113 = bf16[288,2304]{1,0:T(8,128)(2,1)S(1)} collective-permute-done((bf16[288,2304]{1,0:T(8,128)(2,1)S(1)}, bf16[288,2304]{1,0:T(8,128)(2,1)S(1)}, u32[]{:S(2)}, u32[]{:S(2)}) %collective-permute-start.113) | collective-permute-done | bytes 1327136 | tf_op jit(solution)/shard_map/ppermute | solution.py:138
  574.3 5.2 collective-permute-start.87
  582.8 3.8 collective-permute-done.88
  586.6 3.9 collective-permute-start.115
  591.8 5.7 collective-permute-done.120
  604.6 7.1 collective-permute-done.114
  621.3 3.2 multiply_convert_fusion
  631.3 3.8 collective-permute-start.94
  636.1 2.9 convolution_convert_fusion.3
  641.6 6.4 collective-permute-done.94
  652.5 6.3 collective-permute-done.110
  658.8 4.4 collective-permute-start.96
  664.4 8.6 %collective-permute-done.96 = bf16[128,2304]{1,0:T(8,128)(2,1)S(1)} collective-permute-done((bf16[128,2304]{1,0:T(8,128)(2,1)S(1)}, bf16[128,2304]{1,0:T(8,128)(2,1)S(1)}, u32[]{:S(2)}, u32[]{:S(2)}) %collective-permute-start.96) | collective-permute-done | bytes 589856 | tf_op jit(solution)/shard_map/ppermute | solution.py:70
  673.9 11.6 %collective-permute-start.97 = (bf16[128,2304]{1,0:T(8,128)(2,1)S(1)}, bf16[128,2304]{1,0:T(8,128)(2,1)S(1)}, u32[]{:S(2)}, u32[]{:S(2)}) collective-permute-start(bf16[128,2304]{1,0:T(8,128)(2,1)S(1)} %get-tuple-element.99), channel_id=1, source_target_pairs={{0,2},{1,3},{2,4},{3,5},{4,6},{5,7},{8,10},{9,11},{10,12},{11,13},... | collective-permute-start | bytes 1769480 | tf_op jit(solution)/shard_map/ppermute | solution.py:70
  692.9 3.9 collective-permute-start.102
  696.9 3.3 convert_add_fusion.2
  702.0 4.6 collective-permute-done.101
  706.6 11.2 %collective-permute-done.103 = bf16[4,72,1024]{2,1,0:T(8,128)(2,1)S(1)} collective-permute-done((bf16[4,72,1024]{2,1,0:T(8,128)(2,1)S(1)}, bf16[4,72,1024]{2,1,0:T(8,128)(2,1)S(1)}, u32[]{:S(2)}, u32[]{:S(2)}) %collective-permute-start.103) | collective-permute-done | bytes 589856 | tf_op jit(solution)/shard_map/ppermute | solution.py:138
  717.9 4.1 collective-permute-done.102
  722.7 3.9 collective-permute-start.104
  730.8 9.0 %collective-permute-done.105 = bf16[72,1024]{1,0:T(8,128)(2,1)S(1)} collective-permute-done((bf16[72,1024]{1,0:T(8,128)(2,1)S(1)}, bf16[72,1024]{1,0:T(8,128)(2,1)S(1)}, u32[]{:S(2)}, u32[]{:S(2)}) %collective-permute-start.105) | collective-permute-done | bytes 147488 | tf_op jit(solution)/shard_map/ppermute | solution.py:125
  (636 shorter events, 263.4 us)
Async XLA Ops:
  1.4 19.2 %collective-permute-start.2 = (bf16[4,32,72]{2,0,1:T(4,128)(2,1)S(1)}, bf16[4,32,72]{2,0,1:T(4,128)(2,1)S(1)}, u32[]{:S(2)}, u32[]{:S(2)}) collective-permute-start(bf16[4,32,72]{2,0,1:T(4,128)(2,1)S(1)} %constant_dynamic-update-slice_fusion.29), channel_id=1, source_target_pairs={{6,0},{7,1},{0,2},{1,3},{2,4},{3,5},{4,6},{5,7},{14,8},{15,9},{8,1... | collective-permute-start | bytes 55304 | tf_op jit(solution)/shard_map/ppermute | solution.py:125
  4.5 16.1 %collective-permute-start.1 = (bf16[4,32,72]{2,0,1:T(4,128)(2,1)S(1)}, bf16[4,32,72]{2,0,1:T(4,128)(2,1)S(1)}, u32[]{:S(2)}, u32[]{:S(2)}) collective-permute-start(bf16[4,32,72]{2,0,1:T(4,128)(2,1)S(1)} %constant_dynamic-update-slice_fusion.29), channel_id=1, source_target_pairs={{4,0},{5,1},{6,2},{7,3},{0,4},{1,5},{2,6},{3,7},{12,8},{13,9},{14,... | collective-permute-start | bytes 55304 | tf_op jit(solution)/shard_map/ppermute | solution.py:125
  8.4 41.8 %collective-permute-start.24 = (bf16[64,2304]{1,0:T(8,128)(2,1)}, bf16[64,2304]{1,0:T(8,128)(2,1)}, u32[]{:S(2)}, u32[]{:S(2)}) collective-permute-start(bf16[64,2304]{1,0:T(8,128)(2,1)} %param.26), channel_id=1, source_target_pairs={{0,0},{4,1},{8,2},{12,3},{16,4},{20,5},{24,6},{28,7},{1,8},{5,9},{... | collective-permute-start | bytes 884744 | tf_op jit(solution)/shard_map/ppermute | solution.py:285
  17.7 24.3 %collective-permute-start.7 = (bf16[72,1024]{1,0:T(8,128)(2,1)S(1)}, bf16[72,1024]{1,0:T(8,128)(2,1)S(1)}, u32[]{:S(2)}, u32[]{:S(2)}) collective-permute-start(bf16[72,1024]{1,0:T(8,128)(2,1)S(1)} %bitcast.273), channel_id=1, source_target_pairs={{2,0},{3,1},{4,2},{5,3},{6,4},{7,5},{0,6},{1,7},{10,8},{11,9},{12,... | collective-permute-start | bytes 442376 | tf_op jit(solution)/shard_map/ppermute | solution.py:125
  25.9 18.6 %collective-permute-start.8 = (bf16[72,1024]{1,0:T(8,128)(2,1)S(1)}, bf16[72,1024]{1,0:T(8,128)(2,1)S(1)}, u32[]{:S(2)}, u32[]{:S(2)}) collective-permute-start(bf16[72,1024]{1,0:T(8,128)(2,1)S(1)} %bitcast.275), channel_id=1, source_target_pairs={{4,0},{5,1},{6,2},{7,3},{0,4},{1,5},{2,6},{3,7},{12,8},{13,9},{14,... | collective-permute-start | bytes 442376 | tf_op jit(solution)/shard_map/ppermute | solution.py:125
  27.0 17.8 %collective-permute-start.9 = (bf16[72,1024]{1,0:T(8,128)(2,1)S(1)}, bf16[72,1024]{1,0:T(8,128)(2,1)S(1)}, u32[]{:S(2)}, u32[]{:S(2)}) collective-permute-start(bf16[72,1024]{1,0:T(8,128)(2,1)S(1)} %bitcast.274), channel_id=1, source_target_pairs={{6,0},{7,1},{0,2},{1,3},{2,4},{3,5},{4,6},{5,7},{14,8},{15,9},{8,1... | collective-permute-start | bytes 442376 | tf_op jit(solution)/shard_map/ppermute | solution.py:125
  30.1 50.9 %collective-permute-start.18 = (bf16[128,2304]{1,0:T(8,128)(2,1)}, bf16[128,2304]{1,0:T(8,128)(2,1)}, u32[]{:S(2)}, u32[]{:S(2)}) collective-permute-start(bf16[128,2304]{1,0:T(8,128)(2,1)} %multiply_convert_fusion.12), channel_id=1, source_target_pairs={{2,0},{3,1},{4,2},{5,3},{6,4},{7,5},{10,8},{11,9},{12,10},{13,11},... | collective-permute-start | bytes 1769480 | tf_op jit(solution)/shard_map/ppermute | solution.py:70
  42.0 39.0 %collective-permute-start.17 = (bf16[128,2304]{1,0:T(8,128)(2,1)}, bf16[128,2304]{1,0:T(8,128)(2,1)}, u32[]{:S(2)}, u32[]{:S(2)}) collective-permute-start(bf16[128,2304]{1,0:T(8,128)(2,1)} %multiply_convert_fusion.12), channel_id=1, source_target_pairs={{0,2},{1,3},{2,4},{3,5},{4,6},{5,7},{8,10},{9,11},{10,12},{11,13},... | collective-permute-start | bytes 1769480 | tf_op jit(solution)/shard_map/ppermute | solution.py:70
  49.2 22.1 %collective-permute-start.11 = (bf16[4,72,1024]{2,0,1:T(4,128)(2,1)S(1)}, bf16[4,72,1024]{2,0,1:T(4,128)(2,1)S(1)}, u32[]{:S(2)}, u32[]{:S(2)}) collective-permute-start(bf16[4,72,1024]{2,0,1:T(4,128)(2,1)S(1)} %constant_dynamic-slice_fusion.1), channel_id=1, source_target_pairs={{0,8},{8,0},{16,24},{24,16},{1,9},{9,1},{17,25},{25,17},{2,10},{10... | collective-permute-start | bytes 1769480 | tf_op jit(solution)/shard_map/ppermute | solution.py:138
  49.3 21.7 %collective-permute-start.10 = (bf16[4,72,1024]{2,0,1:T(4,128)(2,1)S(1)}, bf16[4,72,1024]{2,0,1:T(4,128)(2,1)S(1)}, u32[]{:S(2)}, u32[]{:S(2)}) collective-permute-start(bf16[4,72,1024]{2,0,1:T(4,128)(2,1)S(1)} %constant_dynamic-slice_fusion.1), channel_id=1, source_target_pairs={{0,1},{1,0},{2,3},{3,2},{4,5},{5,4},{6,7},{7,6},{8,9},{9,8},{10,11... | collective-permute-start | bytes 1769480 | tf_op jit(solution)/shard_map/ppermute | solution.py:73
  52.2 18.8 %collective-permute-start.26 = (bf16[64,2304]{1,0:T(8,128)(2,1)}, bf16[64,2304]{1,0:T(8,128)(2,1)S(1)}, u32[]{:S(2)}, u32[]{:S(2)}) collective-permute-start(bf16[64,2304]{1,0:T(8,128)(2,1)} %collective-permute-done.24), channel_id=1, source_target_pairs={{0,8},{8,0},{16,24},{24,16},{1,9},{9,1},{17,25},{25,17},{2,10},{10... | collective-permute-start | bytes 884744 | tf_op jit(solution)/shard_map/ppermute | solution.py:138
  71.3 22.4 %collective-permute-start.13 = (bf16[4,72,1024]{2,0,1:T(4,128)(2,1)S(1)}, bf16[4,72,1024]{2,0,1:T(4,128)(2,1)S(1)}, u32[]{:S(2)}, u32[]{:S(2)}) collective-permute-start(bf16[4,72,1024]{2,0,1:T(4,128)(2,1)S(1)} %constant_dynamic-slice_fusion.1), channel_id=1, source_target_pairs={{0,16},{8,24},{16,0},{24,8},{1,17},{9,25},{17,1},{25,9},{2,18},{10... | collective-permute-start | bytes 1769480 | tf_op jit(solution)/shard_map/ppermute | solution.py:138
  81.0 19.0 %collective-permute-start.30 = (bf16[64,2304]{1,0:T(8,128)(2,1)S(1)}, bf16[64,2304]{1,0:T(8,128)(2,1)S(1)}, u32[]{:S(2)}, u32[]{:S(2)}) collective-permute-start(bf16[64,2304]{1,0:T(8,128)(2,1)S(1)} %collective-permute-done.26), channel_id=1, source_target_pairs={{0,16},{8,24},{16,0},{24,8},{1,17},{9,25},{17,1},{25,9},{2,18},{10... | collective-permute-start | bytes 884744 | tf_op jit(solution)/shard_map/ppermute | solution.py:138
  81.1 19.0 %collective-permute-start.20 = (bf16[128,2304]{1,0:T(8,128)(2,1)}, bf16[128,2304]{1,0:T(8,128)(2,1)S(1)}, u32[]{:S(2)}, u32[]{:S(2)}) collective-permute-start(bf16[128,2304]{1,0:T(8,128)(2,1)} %collective-permute-done.18), channel_id=1, source_target_pairs={{2,0},{3,1},{4,2},{5,3},{10,8},{11,9},{12,10},{13,11},{18,16},{19,... | collective-permute-start | bytes 1769480 | tf_op jit(solution)/shard_map/ppermute | solution.py:70
  82.4 18.2 %collective-permute-start.19 = (bf16[128,2304]{1,0:T(8,128)(2,1)}, bf16[128,2304]{1,0:T(8,128)(2,1)S(1)}, u32[]{:S(2)}, u32[]{:S(2)}) collective-permute-start(bf16[128,2304]{1,0:T(8,128)(2,1)} %collective-permute-done.17), channel_id=1, source_target_pairs={{2,4},{3,5},{4,6},{5,7},{10,12},{11,13},{12,14},{13,15},{18,20},{1... | collective-permute-start | bytes 1769480 | tf_op jit(solution)/shard_map/ppermute | solution.py:70
  83.2 27.8 %collective-permute-start.15 = (bf16[4,72,1024]{2,0,1:T(4,128)(2,1)S(1)}, bf16[4,72,1024]{2,0,1:T(4,128)(2,1)S(1)}, u32[]{:S(2)}, u32[]{:S(2)}) collective-permute-start(bf16[4,72,1024]{2,0,1:T(4,128)(2,1)S(1)} %collective-permute-done.11), channel_id=1, source_target_pairs={{0,16},{8,24},{16,0},{24,8},{1,17},{9,25},{17,1},{25,9},{2,18},{10... | collective-permute-start | bytes 1769480 | tf_op jit(solution)/shard_map/ppermute | solution.py:138
  100.0 23.1 %collective-permute-start.31 = (bf16[64,2304]{1,0:T(8,128)(2,1)S(1)}, bf16[64,2304]{1,0:T(8,128)(2,1)S(1)}, u32[]{:S(2)}, u32[]{:S(2)}) collective-permute-start(bf16[64,2304]{1,0:T(8,128)(2,1)S(1)} %collective-permute-done.30), channel_id=1, source_target_pairs={{0,1},{1,0},{2,3},{3,2},{4,5},{5,4},{6,7},{7,6},{8,9},{9,8},{10,11... | collective-permute-start | bytes 884744 | tf_op jit(solution)/shard_map/ppermute | solution.py:73
  100.6 17.1 %collective-permute-start.22 = (bf16[128,2304]{1,0:T(8,128)(2,1)S(1)}, bf16[128,2304]{1,0:T(8,128)(2,1)S(1)}, u32[]{:S(2)}, u32[]{:S(2)}) collective-permute-start(bf16[128,2304]{1,0:T(8,128)(2,1)S(1)} %collective-permute-done.20), channel_id=1, source_target_pairs={{2,0},{3,1},{10,8},{11,9},{18,16},{19,17},{26,24},{27,25}} | collective-permute-start | bytes 1769480 | tf_op jit(solution)/shard_map/ppermute | solution.py:70
  131.6 32.5 %collective-permute-start.39 = (bf16[288,2304]{1,0:T(8,128)(2,1)}, bf16[288,2304]{1,0:T(8,128)(2,1)}, u32[]{:S(2)}, u32[]{:S(2)}) collective-permute-start(bf16[288,2304]{1,0:T(8,128)(2,1)} %param.27), channel_id=1, source_target_pairs={{0,8},{8,0},{16,24},{24,16},{1,9},{9,1},{17,25},{25,17},{2,10},{10... | collective-permute-start | bytes 3981320 | tf_op jit(solution)/shard_map/ppermute | solution.py:138
  132.0 35.5 %collective-permute-start.40 = (bf16[288,2304]{1,0:T(8,128)(2,1)}, bf16[288,2304]{1,0:T(8,128)(2,1)}, u32[]{:S(2)}, u32[]{:S(2)}) collective-permute-start(bf16[288,2304]{1,0:T(8,128)(2,1)} %param.27), channel_id=1, source_target_pairs={{0,16},{8,24},{16,0},{24,8},{1,17},{9,25},{17,1},{25,9},{2,18},{10... | collective-permute-start | bytes 3981320 | tf_op jit(solution)/shard_map/ppermute | solution.py:138
  132.8 59.7 %collective-permute-start.42 = (bf16[288,2304]{1,0:T(8,128)(2,1)}, bf16[288,2304]{1,0:T(8,128)(2,1)}, u32[]{:S(2)}, u32[]{:S(2)}) collective-permute-start(bf16[288,2304]{1,0:T(8,128)(2,1)} %param.28), channel_id=1, source_target_pairs={{0,8},{8,0},{16,24},{24,16},{1,9},{9,1},{17,25},{25,17},{2,10},{10... | collective-permute-start | bytes 3981320 | tf_op jit(solution)/shard_map/ppermute | solution.py:138
  137.0 17.5 %collective-permute-start.35 = (bf16[128,2304]{1,0:T(8,128)(2,1)S(1)}, bf16[128,2304]{1,0:T(8,128)(2,1)S(1)}, u32[]{:S(2)}, u32[]{:S(2)}) collective-permute-start(bf16[128,2304]{1,0:T(8,128)(2,1)S(1)} %slice.524), channel_id=1, source_target_pairs={{6,4},{7,5},{14,12},{15,13},{22,20},{23,21},{30,28},{31,29}} | collective-permute-start | bytes 1769480 | tf_op jit(solution)/shard_map/ppermute | solution.py:70
  144.8 16.8 %collective-permute-start.33 = (bf16[128,2304]{1,0:T(8,128)(2,1)S(1)}, bf16[128,2304]{1,0:T(8,128)(2,1)S(1)}, u32[]{:S(2)}, u32[]{:S(2)}) collective-permute-start(bf16[128,2304]{1,0:T(8,128)(2,1)S(1)} %add_convert_fusion.19), channel_id=1, source_target_pairs={{0,2},{1,3},{2,4},{3,5},{8,10},{9,11},{10,12},{11,13},{16,18},{17,... | collective-permute-start | bytes 1769480 | tf_op jit(solution)/shard_map/ppermute | solution.py:70
  154.5 41.8 %collective-permute-start.43 = (bf16[288,2304]{1,0:T(8,128)(2,1)}, bf16[288,2304]{1,0:T(8,128)(2,1)S(1)}, u32[]{:S(2)}, u32[]{:S(2)}) collective-permute-start(bf16[288,2304]{1,0:T(8,128)(2,1)} %param.28), channel_id=1, source_target_pairs={{0,16},{8,24},{16,0},{24,8},{1,17},{9,25},{17,1},{25,9},{2,18},{10... | collective-permute-start | bytes 3981320 | tf_op jit(solution)/shard_map/ppermute | solution.py:138
  161.6 59.2 %collective-permute-start.45 = (bf16[288,2304]{1,0:T(8,128)(2,1)}, bf16[288,2304]{1,0:T(8,128)(2,1)S(1)}, u32[]{:S(2)}, u32[]{:S(2)}) collective-permute-start(bf16[288,2304]{1,0:T(8,128)(2,1)} %param.29), channel_id=1, source_target_pairs={{0,8},{8,0},{16,24},{24,16},{1,9},{9,1},{17,25},{25,17},{2,10},{10... | collective-permute-start | bytes 3981320 | tf_op jit(solution)/shard_map/ppermute | solution.py:138
  167.5 54.8 %collective-permute-start.46 = (bf16[288,2304]{1,0:T(8,128)(2,1)S(1)}, bf16[288,2304]{1,0:T(8,128)(2,1)S(1)}, u32[]{:S(2)}, u32[]{:S(2)}) collective-permute-start(bf16[288,2304]{1,0:T(8,128)(2,1)S(1)} %copy-done.18), channel_id=1, source_target_pairs={{0,16},{8,24},{16,0},{24,8},{1,17},{9,25},{17,1},{25,9},{2,18},{10... | collective-permute-start | bytes 3981320 | tf_op jit(solution)/shard_map/ppermute | solution.py:138
  170.8 27.5 %collective-permute-start.34 = (bf16[128,2304]{1,0:T(8,128)(2,1)S(1)}, bf16[128,2304]{1,0:T(8,128)(2,1)S(1)}, u32[]{:S(2)}, u32[]{:S(2)}) collective-permute-start(bf16[128,2304]{1,0:T(8,128)(2,1)S(1)} %get-tuple-element.103), channel_id=1, source_target_pairs={{0,2},{1,3},{2,4},{3,5},{4,6},{5,7},{8,10},{9,11},{10,12},{11,13},... | collective-permute-start | bytes 1769480 | tf_op jit(solution)/shard_map/ppermute | solution.py:70
  196.3 53.2 %collective-permute-start.41 = (bf16[288,2304]{1,0:T(8,128)(2,1)}, bf16[288,2304]{1,0:T(8,128)(2,1)S(1)}, u32[]{:S(2)}, u32[]{:S(2)}) collective-permute-start(bf16[288,2304]{1,0:T(8,128)(2,1)} %collective-permute-done.39), channel_id=1, source_target_pairs={{0,16},{8,24},{16,0},{24,8},{1,17},{9,25},{17,1},{25,9},{2,18},{10... | collective-permute-start | bytes 3981320 | tf_op jit(solution)/shard_map/ppermute | solution.py:138
  198.3 53.3 %collective-permute-start.44 = (bf16[288,2304]{1,0:T(8,128)(2,1)S(1)}, bf16[288,2304]{1,0:T(8,128)(2,1)S(1)}, u32[]{:S(2)}, u32[]{:S(2)}) collective-permute-start(bf16[288,2304]{1,0:T(8,128)(2,1)S(1)} %collective-permute-done.43), channel_id=1, source_target_pairs={{0,8},{8,0},{16,24},{24,16},{1,9},{9,1},{17,25},{25,17},{2,10},{10... | collective-permute-start | bytes 3981320 | tf_op jit(solution)/shard_map/ppermute | solution.py:138
  208.7 18.4 %collective-permute-start.38 = (bf16[128,2304]{1,0:T(8,128)(2,1)S(1)}, bf16[128,2304]{1,0:T(8,128)(2,1)S(1)}, u32[]{:S(2)}, u32[]{:S(2)}) collective-permute-start(bf16[128,2304]{1,0:T(8,128)(2,1)S(1)} %get-tuple-element.70), channel_id=1, source_target_pairs={{0,1},{1,0},{2,3},{3,2},{4,5},{5,4},{6,7},{7,6},{8,9},{9,8},{10,11... | collective-permute-start | bytes 1769480 | tf_op jit(solution)/shard_map/ppermute | solution.py:73
  227.1 49.7 %collective-permute-start.47 = (bf16[288,2304]{1,0:T(8,128)(2,1)S(1)}, bf16[288,2304]{1,0:T(8,128)(2,1)S(1)}, u32[]{:S(2)}, u32[]{:S(2)}) collective-permute-start(bf16[288,2304]{1,0:T(8,128)(2,1)S(1)} %collective-permute-done.45), channel_id=1, source_target_pairs={{0,16},{8,24},{16,0},{24,8},{1,17},{9,25},{17,1},{25,9},{2,18},{10... | collective-permute-start | bytes 3981320 | tf_op jit(solution)/shard_map/ppermute | solution.py:138
  264.8 16.2 %collective-permute-start.53 = (bf16[128,2304]{1,0:T(8,128)(2,1)S(1)}, bf16[128,2304]{1,0:T(8,128)(2,1)S(1)}, u32[]{:S(2)}, u32[]{:S(2)}) collective-permute-start(bf16[128,2304]{1,0:T(8,128)(2,1)S(1)} %get-tuple-element.66), channel_id=1, source_target_pairs={{0,1},{1,0},{2,3},{3,2},{4,5},{5,4},{6,7},{7,6},{8,9},{9,8},{10,11... | collective-permute-start | bytes 1769480 | tf_op jit(solution)/shard_map/ppermute | solution.py:73
  315.6 20.6 %collective-permute-start.56 = (bf16[128,2304]{1,0:T(8,128)(2,1)S(1)}, bf16[128,2304]{1,0:T(8,128)(2,1)S(1)}, u32[]{:S(2)}, u32[]{:S(2)}) collective-permute-start(bf16[128,2304]{1,0:T(8,128)(2,1)S(1)} %slice.520), channel_id=1, source_target_pairs={{0,1},{1,0},{2,3},{3,2},{4,5},{5,4},{6,7},{7,6},{8,9},{9,8},{10,11... | collective-permute-start | bytes 1769480 | tf_op jit(solution)/shard_map/ppermute | solution.py:73
  324.3 16.6 %collective-permute-start.62 = (bf16[128,2304]{1,0:T(8,128)(2,1)S(1)}, bf16[128,2304]{1,0:T(8,128)(2,1)S(1)}, u32[]{:S(2)}, u32[]{:S(2)}) collective-permute-start(bf16[128,2304]{1,0:T(8,128)(2,1)S(1)} %get-tuple-element.91), channel_id=1, source_target_pairs={{0,2},{1,3},{2,4},{3,5},{8,10},{9,11},{10,12},{11,13},{16,18},{17,... | collective-permute-start | bytes 1769480 | tf_op jit(solution)/shard_map/ppermute | solution.py:70
  336.3 18.9 %collective-permute-start.48 = (bf16[128,2304]{1,0:T(8,128)(2,1)}, bf16[128,2304]{1,0:T(8,128)(2,1)}, u32[]{:S(2)}, u32[]{:S(2)}) collective-permute-start(bf16[128,2304]{1,0:T(8,128)(2,1)} %slice.522), channel_id=1, source_target_pairs={{0,1},{1,0},{2,3},{3,2},{4,5},{5,4},{6,7},{7,6},{8,9},{9,8},{10,11... | collective-permute-start | bytes 1769480 | tf_op jit(solution)/shard_map/ppermute | solution.py:73
  342.4 18.0 %collective-permute-start.63 = (bf16[128,2304]{1,0:T(8,128)(2,1)}, bf16[128,2304]{1,0:T(8,128)(2,1)}, u32[]{:S(2)}, u32[]{:S(2)}) collective-permute-start(bf16[128,2304]{1,0:T(8,128)(2,1)} %get-tuple-element.89), channel_id=1, source_target_pairs={{0,2},{1,3},{2,4},{3,5},{4,6},{5,7},{8,10},{9,11},{10,12},{11,13},... | collective-permute-start | bytes 1769480 | tf_op jit(solution)/shard_map/ppermute | solution.py:70
  370.6 17.3 %collective-permute-start.71 = (bf16[128,2304]{1,0:T(8,128)(2,1)S(1)}, bf16[128,2304]{1,0:T(8,128)(2,1)S(1)}, u32[]{:S(2)}, u32[]{:S(2)}) collective-permute-start(bf16[128,2304]{1,0:T(8,128)(2,1)S(1)} %get-tuple-element.78), channel_id=1, source_target_pairs={{2,0},{3,1},{4,2},{5,3},{6,4},{7,5},{10,8},{11,9},{12,10},{13,11},... | collective-permute-start | bytes 1769480 | tf_op jit(solution)/shard_map/ppermute | solution.py:70
  372.2 16.9 %collective-permute-start.69 = (bf16[128,2304]{1,0:T(8,128)(2,1)S(1)}, bf16[128,2304]{1,0:T(8,128)(2,1)S(1)}, u32[]{:S(2)}, u32[]{:S(2)}) collective-permute-start(bf16[128,2304]{1,0:T(8,128)(2,1)S(1)} %get-tuple-element.78), channel_id=1, source_target_pairs={{0,2},{1,3},{2,4},{3,5},{4,6},{5,7},{8,10},{9,11},{10,12},{11,13},... | collective-permute-start | bytes 1769480 | tf_op jit(solution)/shard_map/ppermute | solution.py:70
  394.9 17.5 %collective-permute-start.72 = (bf16[128,2304]{1,0:T(8,128)(2,1)S(1)}, bf16[128,2304]{1,0:T(8,128)(2,1)S(1)}, u32[]{:S(2)}, u32[]{:S(2)}) collective-permute-start(bf16[128,2304]{1,0:T(8,128)(2,1)S(1)} %collective-permute-done.71), channel_id=1, source_target_pairs={{2,0},{3,1},{4,2},{5,3},{10,8},{11,9},{12,10},{13,11},{18,16},{19,... | collective-permute-start | bytes 1769480 | tf_op jit(solution)/shard_map/ppermute | solution.py:70
  396.2 16.2 %collective-permute-start.70 = (bf16[128,2304]{1,0:T(8,128)(2,1)S(1)}, bf16[128,2304]{1,0:T(8,128)(2,1)S(1)}, u32[]{:S(2)}, u32[]{:S(2)}) collective-permute-start(bf16[128,2304]{1,0:T(8,128)(2,1)S(1)} %collective-permute-done.69), channel_id=1, source_target_pairs={{2,4},{3,5},{4,6},{5,7},{10,12},{11,13},{12,14},{13,15},{18,20},{1... | collective-permute-start | bytes 1769480 | tf_op jit(solution)/shard_map/ppermute | solution.py:70
  399.6 110.5 %collective-permute-start.68 = (bf16[128,2304]{1,0:T(8,128)(2,1)}, bf16[128,2304]{1,0:T(8,128)(2,1)}, u32[]{:S(2)}, u32[]{:S(2)}) collective-permute-start(bf16[128,2304]{1,0:T(8,128)(2,1)} %slice.518), channel_id=1, source_target_pairs={{0,1},{1,0},{2,3},{3,2},{4,5},{5,4},{6,7},{7,6},{8,9},{9,8},{10,11... | collective-permute-start | bytes 1769480 | tf_op jit(solution)/shard_map/ppermute | solution.py:73
  417.5 18.2 %collective-permute-start.78 = (bf16[128,2304]{1,0:T(8,128)(2,1)S(1)}, bf16[128,2304]{1,0:T(8,128)(2,1)S(1)}, u32[]{:S(2)}, u32[]{:S(2)}) collective-permute-start(bf16[128,2304]{1,0:T(8,128)(2,1)S(1)} %collective-permute-done.72), channel_id=1, source_target_pairs={{2,0},{3,1},{10,8},{11,9},{18,16},{19,17},{26,24},{27,25}} | collective-permute-start | bytes 1769480 | tf_op jit(solution)/shard_map/ppermute | solution.py:70
  418.8 16.9 %collective-permute-start.77 = (bf16[128,2304]{1,0:T(8,128)(2,1)S(1)}, bf16[128,2304]{1,0:T(8,128)(2,1)S(1)}, u32[]{:S(2)}, u32[]{:S(2)}) collective-permute-start(bf16[128,2304]{1,0:T(8,128)(2,1)S(1)} %collective-permute-done.70), channel_id=1, source_target_pairs={{4,6},{5,7},{12,14},{13,15},{20,22},{21,23},{28,30},{29,31}} | collective-permute-start | bytes 1769480 | tf_op jit(solution)/shard_map/ppermute | solution.py:70
  421.7 62.7 %collective-permute-start.76 = (bf16[128,2304]{1,0:T(8,128)(2,1)S(1)}, bf16[128,2304]{1,0:T(8,128)(2,1)S(1)}, u32[]{:S(2)}, u32[]{:S(2)}) collective-permute-start(bf16[128,2304]{1,0:T(8,128)(2,1)S(1)} %slice.516), channel_id=1, source_target_pairs={{0,1},{1,0},{2,3},{3,2},{4,5},{5,4},{6,7},{7,6},{8,9},{9,8},{10,11... | collective-permute-start | bytes 1769480 | tf_op jit(solution)/shard_map/ppermute | solution.py:73
  444.2 22.5 %collective-permute-start.74 = (bf16[128,2304]{1,0:T(8,128)(2,1)S(1)}, bf16[128,2304]{1,0:T(8,128)(2,1)S(1)}, u32[]{:S(2)}, u32[]{:S(2)}) collective-permute-start(bf16[128,2304]{1,0:T(8,128)(2,1)S(1)} %slice.517), channel_id=1, source_target_pairs={{0,1},{1,0},{2,3},{3,2},{4,5},{5,4},{6,7},{7,6},{8,9},{9,8},{10,11... | collective-permute-start | bytes 1769480 | tf_op jit(solution)/shard_map/ppermute | solution.py:73
  466.7 107.7 %collective-permute-start.118 = (bf16[288,2304]{1,0:T(8,128)(2,1)S(1)}, bf16[288,2304]{1,0:T(8,128)(2,1)S(1)}, u32[]{:S(2)}, u32[]{:S(2)}) collective-permute-start(bf16[288,2304]{1,0:T(8,128)(2,1)S(1)} %get-tuple-element.93), channel_id=1, source_target_pairs={{0,16},{8,24},{16,0},{24,8},{1,17},{9,25},{17,1},{25,9},{2,18},{10... | collective-permute-start | bytes 3981320 | tf_op jit(solution)/shard_map/ppermute | solution.py:138
  470.5 16.5 %collective-permute-start.83 = (bf16[128,2304]{1,0:T(8,128)(2,1)S(1)}, bf16[128,2304]{1,0:T(8,128)(2,1)S(1)}, u32[]{:S(2)}, u32[]{:S(2)}) collective-permute-start(bf16[128,2304]{1,0:T(8,128)(2,1)S(1)} %get-tuple-element.33), channel_id=1, source_target_pairs={{0,2},{1,3},{2,4},{3,5},{8,10},{9,11},{10,12},{11,13},{16,18},{17,... | collective-permute-start | bytes 1769480 | tf_op jit(solution)/shard_map/ppermute | solution.py:70
  484.3 41.8 %collective-permute-start.119 = (bf16[288,2304]{1,0:T(8,128)(2,1)S(1)}, bf16[288,2304]{1,0:T(8,128)(2,1)S(1)}, u32[]{:S(2)}, u32[]{:S(2)}) collective-permute-start(bf16[288,2304]{1,0:T(8,128)(2,1)S(1)} %get-tuple-element.94), channel_id=1, source_target_pairs={{0,16},{8,24},{16,0},{24,8},{1,17},{9,25},{17,1},{25,9},{2,18},{10... | collective-permute-start | bytes 3981320 | tf_op jit(solution)/shard_map/ppermute | solution.py:138
  488.3 23.4 %collective-permute-start.85 = (bf16[128,2304]{1,0:T(8,128)(2,1)}, bf16[128,2304]{1,0:T(8,128)(2,1)S(1)}, u32[]{:S(2)}, u32[]{:S(2)}) collective-permute-start(bf16[128,2304]{1,0:T(8,128)(2,1)} %get-tuple-element.35), channel_id=1, source_target_pairs={{0,2},{1,3},{2,4},{3,5},{4,6},{5,7},{8,10},{9,11},{10,12},{11,13},... | collective-permute-start | bytes 1769480 | tf_op jit(solution)/shard_map/ppermute | solution.py:70
  510.1 94.5 %collective-permute-start.112 = (bf16[288,2304]{1,0:T(8,128)(2,1)S(1)}, bf16[288,2304]{1,0:T(8,128)(2,1)S(1)}, u32[]{:S(2)}, u32[]{:S(2)}) collective-permute-start(bf16[288,2304]{1,0:T(8,128)(2,1)S(1)} %get-tuple-element.97), channel_id=1, source_target_pairs={{0,8},{8,0},{16,24},{24,16},{1,9},{9,1},{17,25},{25,17},{2,10},{10... | collective-permute-start | bytes 3981320 | tf_op jit(solution)/shard_map/ppermute | solution.py:138
  540.7 32.0 %collective-permute-start.113 = (bf16[288,2304]{1,0:T(8,128)(2,1)S(1)}, bf16[288,2304]{1,0:T(8,128)(2,1)S(1)}, u32[]{:S(2)}, u32[]{:S(2)}) collective-permute-start(bf16[288,2304]{1,0:T(8,128)(2,1)S(1)} %get-tuple-element.98), channel_id=1, source_target_pairs={{0,8},{8,0},{16,24},{24,16},{1,9},{9,1},{17,25},{25,17},{2,10},{10... | collective-permute-start | bytes 3981320 | tf_op jit(solution)/shard_map/ppermute | solution.py:138
  542.3 37.2 %collective-permute-start.116 = (bf16[288,2304]{1,0:T(8,128)(2,1)S(1)}, bf16[288,2304]{1,0:T(8,128)(2,1)S(1)}, u32[]{:S(2)}, u32[]{:S(2)}) collective-permute-start(bf16[288,2304]{1,0:T(8,128)(2,1)S(1)} %get-tuple-element.96), channel_id=1, source_target_pairs={{0,16},{8,24},{16,0},{24,8},{1,17},{9,25},{17,1},{25,9},{2,18},{10... | collective-permute-start | bytes 3981320 | tf_op jit(solution)/shard_map/ppermute | solution.py:138
  545.4 52.1 %collective-permute-start.120 = (bf16[288,2304]{1,0:T(8,128)(2,1)S(1)}, bf16[288,2304]{1,0:T(8,128)(2,1)S(1)}, u32[]{:S(2)}, u32[]{:S(2)}) collective-permute-start(bf16[288,2304]{1,0:T(8,128)(2,1)S(1)} %add_convert_fusion), channel_id=1, source_target_pairs={{0,8},{8,0},{16,24},{24,16},{1,9},{9,1},{17,25},{25,17},{2,10},{10... | collective-permute-start | bytes 3981320 | tf_op jit(solution)/shard_map/ppermute | solution.py:138
  574.3 16.2 %collective-permute-start.87 = (bf16[128,2304]{1,0:T(8,128)(2,1)S(1)}, bf16[128,2304]{1,0:T(8,128)(2,1)S(1)}, u32[]{:S(2)}, u32[]{:S(2)}) collective-permute-start(bf16[128,2304]{1,0:T(8,128)(2,1)S(1)} %multiply_convert_fusion.1), channel_id=1, source_target_pairs={{0,2},{1,3},{2,4},{3,5},{4,6},{5,7},{8,10},{9,11},{10,12},{11,13},... | collective-permute-start | bytes 1769480 | tf_op jit(solution)/shard_map/ppermute | solution.py:70
  579.6 32.1 %collective-permute-start.114 = (bf16[288,2304]{1,0:T(8,128)(2,1)S(1)}, bf16[288,2304]{1,0:T(8,128)(2,1)S(1)}, u32[]{:S(2)}, u32[]{:S(2)}) collective-permute-start(bf16[288,2304]{1,0:T(8,128)(2,1)S(1)} %add_convert_fusion.2), channel_id=1, source_target_pairs={{0,16},{8,24},{16,0},{24,8},{1,17},{9,25},{17,1},{25,9},{2,18},{10... | collective-permute-start | bytes 3981320 | tf_op jit(solution)/shard_map/ppermute | solution.py:138
  586.6 102.1 %collective-permute-start.115 = (bf16[288,2304]{1,0:T(8,128)(2,1)}, bf16[288,2304]{1,0:T(8,128)(2,1)}, u32[]{:S(2)}, u32[]{:S(2)}) collective-permute-start(bf16[288,2304]{1,0:T(8,128)(2,1)} %get-tuple-element.95), channel_id=1, source_target_pairs={{0,16},{8,24},{16,0},{24,8},{1,17},{9,25},{17,1},{25,9},{2,18},{10... | collective-permute-start | bytes 3981320 | tf_op jit(solution)/shard_map/ppermute | solution.py:138
  631.3 16.6 %collective-permute-start.94 = (bf16[128,2304]{1,0:T(8,128)(2,1)S(1)}, bf16[128,2304]{1,0:T(8,128)(2,1)S(1)}, u32[]{:S(2)}, u32[]{:S(2)}) collective-permute-start(bf16[128,2304]{1,0:T(8,128)(2,1)S(1)} %slice.523), channel_id=1, source_target_pairs={{0,2},{1,3},{8,10},{9,11},{16,18},{17,19},{24,26},{25,27}} | collective-permute-start | bytes 1769480 | tf_op jit(solution)/shard_map/ppermute | solution.py:70
  639.3 46.2 %collective-permute-start.100 = (bf16[4,4,72,1024]{3,2,1,0:T(8,128)(2,1)S(1)}, bf16[4,4,72,1024]{3,2,1,0:T(8,128)(2,1)S(1)}, u32[]{:S(2)}, u32[]{:S(2)}) collective-permute-start(bf16[4,4,72,1024]{3,2,1,0:T(8,128)(2,1)S(1)} %fusion.1), channel_id=1, source_target_pairs={{0,1},{1,0},{2,3},{3,2},{4,5},{5,4},{6,7},{7,6},{8,9},{9,8},{10,11... | collective-permute-start | bytes 7077896 | tf_op jit(solution)/shard_map/ppermute | solution.py:73
  652.1 40.8 %collective-permute-start.117 = (bf16[288,2304]{1,0:T(8,128)(2,1)S(1)}, bf16[288,2304]{1,0:T(8,128)(2,1)S(1)}, u32[]{:S(2)}, u32[]{:S(2)}) collective-permute-start(bf16[288,2304]{1,0:T(8,128)(2,1)S(1)} %copy-done.19), channel_id=1, source_target_pairs={{0,8},{8,0},{16,24},{24,16},{1,9},{9,1},{17,25},{25,17},{2,10},{10... | collective-permute-start | bytes 3981320 | tf_op jit(solution)/shard_map/ppermute | solution.py:138
  672.9 20.0 %collective-permute-start.111 = (bf16[64,2304]{1,0:T(8,128)(2,1)S(1)}, bf16[64,2304]{1,0:T(8,128)(2,1)S(1)}, u32[]{:S(2)}, u32[]{:S(2)}) collective-permute-start(bf16[64,2304]{1,0:T(8,128)(2,1)S(1)} %fusion.86), channel_id=1, source_target_pairs={{0,0},{1,4},{2,8},{3,12},{4,16},{5,20},{6,24},{7,28},{8,1},{9,5},{... | collective-permute-start | bytes 884744 | tf_op jit(solution)/shard_map/ppermute | solution.py:469
  673.9 27.2 %collective-permute-start.97 = (bf16[128,2304]{1,0:T(8,128)(2,1)S(1)}, bf16[128,2304]{1,0:T(8,128)(2,1)S(1)}, u32[]{:S(2)}, u32[]{:S(2)}) collective-permute-start(bf16[128,2304]{1,0:T(8,128)(2,1)S(1)} %get-tuple-element.99), channel_id=1, source_target_pairs={{0,2},{1,3},{2,4},{3,5},{4,6},{5,7},{8,10},{9,11},{10,12},{11,13},... | collective-permute-start | bytes 1769480 | tf_op jit(solution)/shard_map/ppermute | solution.py:70
  688.7 17.9 %collective-permute-start.101 = (bf16[4,72,1024]{2,1,0:T(8,128)(2,1)S(1)}, bf16[4,72,1024]{2,1,0:T(8,128)(2,1)S(1)}, u32[]{:S(2)}, u32[]{:S(2)}) collective-permute-start(bf16[4,72,1024]{2,1,0:T(8,128)(2,1)S(1)} %get-tuple-element.105), channel_id=1, source_target_pairs={{0,8},{8,0},{16,24},{24,16},{1,9},{9,1},{17,25},{25,17},{2,10},{10... | collective-permute-start | bytes 1769480 | tf_op jit(solution)/shard_map/ppermute | solution.py:138
  692.9 24.9 %collective-permute-start.103 = (bf16[4,72,1024]{2,1,0:T(8,128)(2,1)S(1)}, bf16[4,72,1024]{2,1,0:T(8,128)(2,1)S(1)}, u32[]{:S(2)}, u32[]{:S(2)}) collective-permute-start(bf16[4,72,1024]{2,1,0:T(8,128)(2,1)S(1)} %get-tuple-element.106), channel_id=1, source_target_pairs={{0,24},{8,16},{16,8},{24,0},{1,25},{9,17},{17,9},{25,1},{2,26},{10... | collective-permute-start | bytes 1769480 | tf_op jit(solution)/shard_map/ppermute | solution.py:138
  692.9 29.0 %collective-permute-start.102 = (bf16[4,72,1024]{2,1,0:T(8,128)(2,1)S(1)}, bf16[4,72,1024]{2,1,0:T(8,128)(2,1)S(1)}, u32[]{:S(2)}, u32[]{:S(2)}) collective-permute-start(bf16[4,72,1024]{2,1,0:T(8,128)(2,1)S(1)} %get-tuple-element.107), channel_id=1, source_target_pairs={{0,16},{8,24},{16,0},{24,8},{1,17},{9,25},{17,1},{25,9},{2,18},{10... | collective-permute-start | bytes 1769480 | tf_op jit(solution)/shard_map/ppermute | solution.py:138
  (172 other events, 1747.6 us)

commit v2 on v1

--- a/solution.py
+++ b/solution.py
@@ -174,10 +174,20 @@
     return [own.astype(F32) + other.astype(F32) for own, other in zip(pieces[:half], sent)]
 
 
-def everywhere(array, line, batch_size):
-    array = sum((line.shift(array, k) for k in range(1, line.size)), array)
-    array = sum((across(array, k, batch_size) for k in range(1, batch_size)), array)
-    return array + line.partner(array)
+def everywhere(array, line, batch_size, rounds):
+    for one in rounds:
+        if one == "line":
+            sent = [line.shift(array, k) for k in range(1, line.size)]
+        elif one == "batch":
+            sent = [across(array, k, batch_size) for k in range(1, batch_size)]
+        else:
+            sent = [line.partner(array)]
+        array = sum(sent, array)
+    return array
+
+
+def batch_pieces(rows, batch_size):
+    return [rows] + [across(rows, k, batch_size) for k in range(1, batch_size)]
 
 
 def on_device(
@@ -230,7 +240,7 @@
     spread = lax.dynamic_update_slice(
         jnp.zeros((4, devices, piece), BF16), own_gains[:, None], (0, flat_index, 0)
     )
-    gains = everywhere(spread, line, batch_size).reshape(4, features)
+    gains = everywhere(spread, line, batch_size, ("batch", "line", "pair")).reshape(4, features)
     gain_one, gain_two, gain_three, gain_four = gains[0], gains[1], gains[2], gains[3]
 
     weight_rows = query_weight.shape[0]
@@ -269,13 +279,14 @@
     def placed(pieces, shape, block):
         whole = jnp.zeros(shape, BF16)
         for k, one in enumerate(pieces):
-            for parity, rows in ((line.parity, one), (1 - line.parity, line.partner(one))):
+            other = line.partner(one)
+            for parity, rows in ((line.parity, one), (1 - line.parity, other)):
                 start, update = block(batch_index ^ k, parity, rows)
                 whole = lax.dynamic_update_slice(whole, update, start)
         return whole
 
     w_half = from_start(jnp.stack(received))
-    pieces = cube_gather(w_half, bits_up, batch_size)
+    pieces = batch_pieces(w_half, batch_size)
     w_qkv = placed(
         pieces,
         (batch_size, line.size, 2) + w_half.shape[1:],
@@ -283,7 +294,7 @@
     ).reshape(features, query_width + 2 * HEAD_DIM)
 
     out_half = lax.ppermute(out_weight, ("batch", "ctx"), owner_pairs)
-    out_pieces = cube_gather(out_half, bits_up, batch_size)
+    out_pieces = batch_pieces(out_half, batch_size)
     w_out = placed(
         out_pieces,
         (2, batch_size) + out_half.shape,
@@ -355,8 +366,8 @@
 
     def forward_work(k, arrived):
         expanded.append(expand(arrived[k - 1]))
-        if k > 1:
-            parts.append(contract(expanded[k - 2]))
+        if k == line.size - 1:
+            parts.extend(contract(forward) for forward in expanded[:-1])
 
     normed_rows, _ = line.gather(normed_m.astype(BF16), forward_work)
     expanded.append(expand(normed_rows[-1]))
@@ -386,29 +397,41 @@
     grad_gate = stack([e[1] for e in shrunk])
     grad_up = stack([e[2] for e in shrunk])
 
-    def unit_grads(left, right, bits):
+    def unit_grads(left, right, orders):
         total = cols_product(left, right).astype(BF16)
-        pieces = [total[i * unit_rows : (i + 1) * unit_rows] for i in cube_order(bits)]
-        return pieces, cube_send(pieces, bits[-1], batch_size)
-
-    def first_sum(pieces, sent, bits):
-        pieces = cube_add(pieces, sent)
-        if len(bits) == 1:
-            return pieces, None
-        return pieces, cube_send(pieces, bits[-2], batch_size)
-
-    def rest(pieces, sent, bits):
-        for bit in reversed(bits[:-1]):
-            sent = cube_send(pieces, bit, batch_size) if sent is None else sent
+        ends = [unit_rows] if len(orders) == 1 else [unit_rows * 5 // 9, unit_rows]
+        sums = []
+        for start, end, bits in zip([0] + ends, ends, orders):
+            pieces = [
+                total[i * unit_rows + start : i * unit_rows + end] for i in cube_order(bits)
+            ]
+            sums.append((pieces, cube_send(pieces, bits[-1], batch_size), bits))
+        return sums
+
+    def first_sum(sums):
+        after = []
+        for pieces, sent, bits in sums:
             pieces, sent = cube_add(pieces, sent), None
-        return pieces[0]
+            if len(bits) > 1:
+                sent = cube_send(pieces, bits[-2], batch_size)
+            after.append((pieces, sent, bits))
+        return after
+
+    def rest(sums):
+        totals = []
+        for pieces, sent, bits in sums:
+            for bit in reversed(bits[:-1]):
+                sent = cube_send(pieces, bit, batch_size) if sent is None else sent
+                pieces, sent = cube_add(pieces, sent), None
+            totals.append(pieces[0])
+        return stack(totals) if len(totals) > 1 else totals[0]
 
     grad_nm, (down_sum, gate_sum, up_sum) = line.scatter(
         [e[3] for e in shrunk],
         (
-            (functools.partial(unit_grads, bits=bits_up), (hidden, ffn_rows)),
-            (functools.partial(unit_grads, bits=bits_down), (grad_gate, mid_rows)),
-            (functools.partial(unit_grads, bits=bits_up), (grad_up, mid_rows)),
+            (functools.partial(unit_grads, orders=(bits_up,)), (hidden, ffn_rows)),
+            (functools.partial(unit_grads, orders=(bits_down,)), (grad_gate, mid_rows)),
+            (functools.partial(unit_grads, orders=(bits_up, bits_down)), (grad_up, mid_rows)),
         ),
     )
 
@@ -417,19 +440,19 @@
     grad_branch, grad_two = norm_back(branch, inv_two, gain_two, grad_mid)
     gain_grads = jnp.stack((grad_two, grad_three, grad_four))
 
-    gain_grads = everywhere(gain_grads, line, batch_size)
+    gain_grads = everywhere(gain_grads, line, batch_size, ("line", "pair", "batch"))
     gain_grads = lax.dynamic_slice_in_dim(gain_grads, flat_index * piece, piece, axis=1)
 
     def back_work(k, arrived):
         if k == line.size - 2:
-            return first_sum(*down_sum, bits_up)
+            return first_sum(down_sum)
         if k == line.size - 1:
-            return first_sum(*gate_sum, bits_down)
+            return first_sum(gate_sum), first_sum(up_sum)
 
     branch_rows, back_results = line.gather(grad_branch.astype(BF16), back_work)
     grad_branch_b = stack(branch_rows)
-    down_grad = rest(*back_results[-2], bits_up)
-    gate_grad = rest(*back_results[-1], bits_down)
+    down_grad = rest(back_results[-2])
+    gate_grad = rest(back_results[-1][0])
     grad_att = by_head(rows_product(grad_branch_b, w_out).astype(BF16))
     delta = jnp.sum(grad_att.astype(F32) * attended.astype(F32), axis=1, keepdims=True)
     prob = raw / totals
@@ -450,15 +473,22 @@
         other = line.partner(jnp.where(even, part_odd, part_even))
         return jnp.where(even, part_even, part_odd), other
 
-    grad_in, (qkv_parts, up_sum) = line.scatter(
+    pair_parts = []
+
+    def qkv_first(rows, grads):
+        pair_parts.extend(qkv_work(rows, grads))
+        return ()
+
+    def qkv_second():
+        part = (pair_parts[0].astype(F32) + pair_parts[1].astype(F32)).astype(BF16)
+        return part
+
+    grad_in, (_, qkv_part) = line.scatter(
         slots(rows_product(grad_qkv, w_qkv)),
-        (
-            (qkv_work, (stack(normed_in), grad_qkv)),
-            (lambda: first_sum(*up_sum, bits_up), ()),
-        ),
-    )
-    up_grad = rest(*up_sum, bits_up)
-    qkv_part = (qkv_parts[0].astype(F32) + qkv_parts[1].astype(F32)).astype(BF16)
+        ((qkv_first, (stack(normed_in), grad_qkv)), (qkv_second, ())),
+    )
+    qkv_part = batch_scatter(qkv_part, batch_index, batch_size)
+    up_grad = rest(back_results[-1][1])
 
     out_part = cols_product(attended_rows, grad_branch_b).reshape(2, -1, features)
     out_other = line.partner(jnp.where(even, out_part[1], out_part[0]).astype(BF16))
@@ -467,10 +497,11 @@
         out_part.astype(BF16).reshape(batch_size, -1, features), batch_index, batch_size
     )
     out_grad = lax.ppermute(
-        out_part.astype(BF16), ("batch", "ctx"), [(there, here) for here, there in owner_pairs]
+        out_part.astype(BF16),
+        ("batch", "ctx"),
+        [(there, here) for here, there in owner_pairs],
     ).astype(F32)
 
-    qkv_part = batch_scatter(qkv_part, batch_index, batch_size)
     turned = from_here(qkv_part.astype(BF16))
     returned = [turned[0]] + [
         line.shift(turned[line.size - k], k) for k in range(1, line.size)

time: 752 us -> 827 us (1.100)
  waiting for transfers between devices: 352 us -> 411 us
  starting transfers between devices: 192 us -> 205 us
  matrix products: 99.4 us -> 109 us
    ppermute x48, waiting for transfers between devices: 150 us -> 179 us  [move(): return lax.ppermute(rows, 'ctx', pairs)]
    ppermute x36 -> x39, waiting for transfers between devices: 174 us -> 196 us  [across(): lax.ppermute(rows, 'batch', [(b, b ^ bit) for b in range(batch_size)])]
    ppermute x12, starting transfers between devices: 19.7 us -> 28.9 us  [shift(): return lax.ppermute(rows, 'ctx', pairs)]
    ppermute x12, waiting for transfers between devices: 22.8 us -> 31.3 us  [shift(): return lax.ppermute(rows, 'ctx', pairs)]
    ppermute x36 -> x39, starting transfers between devices: 43.5 us -> 39.6 us  [across(): lax.ppermute(rows, 'batch', [(b, b ^ bit) for b in range(batch_size)])]
  transfers between devices with their start and end apart: 128 -> 131, of which waited for: 55 -> 57; matrix products, arithmetic and copies ran while one was open for 23% -> 21% of each run, Pallas kernels for 0% -> 0%
where the time goes in v2:
time: 827 us; the launch traced here: 818 us
  waiting for transfers between devices  411 us (50%)
  starting transfers between devices  205 us (25%)
  matrix products  109 us (13%)
  other arithmetic  44.9 us (5%)
  local copies, waits for them, and re-layouts  44.6 us (5%)
    ppermute x39, waiting for transfers between devices, across(): lax.ppermute(rows, 'batch', [(b, b ^ bit) for b in range(batch_size)])  196 us
    ppermute x48, waiting for transfers between devices, move(): return lax.ppermute(rows, 'ctx', pairs)  179 us
    ppermute x48, starting transfers between devices, move(): return lax.ppermute(rows, 'ctx', pairs)  127 us
    ppermute x39, starting transfers between devices, across(): lax.ppermute(rows, 'batch', [(b, b ^ bit) for b in range(batch_size)])  39.6 us
    dot_general x16, matrix products, rows_product(): lax.dot_general(left_mat, right_mat, (((1,), (1,)), ((), ())), preferred_...  39 us
    dot_general x19, matrix products, product(): return jnp.dot(left_mat, right_mat, preferred_element_type=F32)  37.9 us
    dot_general x7, matrix products, cols_product(): lax.dot_general(left_mat, right_mat, (((0,), (0,)), ((), ())), preferred_...  32.2 us
    ppermute x12, waiting for transfers between devices, shift(): return lax.ppermute(rows, 'ctx', pairs)  31.3 us
  transfers between devices with their start and end apart: 131, of which 57 were waited for; matrix products, arithmetic and copies ran while one was open for 21% of the time, Pallas kernels for 0%

profile of v2, /device:TPU:0, one launch (start us, length us, event | category | flops | bytes accessed | tf_op | source)
XLA Modules:
  0.0 818.1 jit_solution(7029157637151544596)
XLA Ops:
  1.4 4.0 collective-permute-start.2
  6.0 3.8 collective-permute-start.24
  25.9 8.0 collective-permute-done.4
  33.9 8.6 %collective-permute-done.3 = bf16[4,32,72]{2,0,1:T(4,128)(2,1)S(1)} collective-permute-done((bf16[4,32,72]{2,0,1:T(4,128)(2,1)S(1)}, bf16[4,32,72]{2,0,1:T(4,128)(2,1)S(1)}, u32[]{:S(2)}, u32[]{:S(2)}) %collective-permute-start.3) | collective-permute-done | bytes 18464 | tf_op jit(solution)/shard_map/ppermute | solution.py:125
  47.0 5.4 collective-permute-start.17
  53.1 3.6 concatenate.103
  62.3 16.5 %collective-permute-done.26 = bf16[64,2304]{1,0:T(8,128)(2,1)S(1)} collective-permute-done((bf16[64,2304]{1,0:T(8,128)(2,1)}, bf16[64,2304]{1,0:T(8,128)(2,1)S(1)}, u32[]{:S(2)}, u32[]{:S(2)}) %collective-permute-start.26) | collective-permute-done | bytes 294944 | tf_op jit(solution)/shard_map/ppermute | solution.py:138
  81.4 13.8 %collective-permute-done.28 = bf16[64,2304]{1,0:T(8,128)(2,1)S(1)} collective-permute-done((bf16[64,2304]{1,0:T(8,128)(2,1)}, bf16[64,2304]{1,0:T(8,128)(2,1)S(1)}, u32[]{:S(2)}, u32[]{:S(2)}) %collective-permute-start.28) | collective-permute-done | bytes 294944 | tf_op jit(solution)/shard_map/ppermute | solution.py:138
  100.3 12.1 %collective-permute-done.30 = bf16[64,2304]{1,0:T(8,128)(2,1)S(1)} collective-permute-done((bf16[64,2304]{1,0:T(8,128)(2,1)}, bf16[64,2304]{1,0:T(8,128)(2,1)S(1)}, u32[]{:S(2)}, u32[]{:S(2)}) %collective-permute-start.30) | collective-permute-done | bytes 294944 | tf_op jit(solution)/shard_map/ppermute | solution.py:138
  112.4 6.1 collective-permute-done.13
  123.4 13.3 %collective-permute-done.22 = bf16[128,2304]{1,0:T(8,128)(2,1)S(1)} collective-permute-done((bf16[128,2304]{1,0:T(8,128)(2,1)S(1)}, bf16[128,2304]{1,0:T(8,128)(2,1)S(1)}, u32[]{:S(2)}, u32[]{:S(2)}) %collective-permute-start.22) | collective-permute-done | bytes 589856 | tf_op jit(solution)/shard_map/ppermute | solution.py:70
  154.9 9.0 %collective-permute-done.32 = bf16[128,2304]{1,0:T(8,128)(2,1)S(1)} collective-permute-done((bf16[128,2304]{1,0:T(8,128)(2,1)}, bf16[128,2304]{1,0:T(8,128)(2,1)S(1)}, u32[]{:S(2)}, u32[]{:S(2)}) %collective-permute-start.32) | collective-permute-done | bytes 589856 | tf_op jit(solution)/shard_map/ppermute | solution.py:70
  164.9 5.2 collective-permute-start.33
  174.9 6.9 collective-permute-done.33
  191.1 13.7 %collective-permute-start.34 = (bf16[128,2304]{1,0:T(8,128)(2,1)S(1)}, bf16[128,2304]{1,0:T(8,128)(2,1)S(1)}, u32[]{:S(2)}, u32[]{:S(2)}) collective-permute-start(bf16[128,2304]{1,0:T(8,128)(2,1)S(1)} %get-tuple-element.105), channel_id=1, source_target_pairs={{0,2},{1,3},{2,4},{3,5},{4,6},{5,7},{8,10},{9,11},{10,12},{11,13},... | collective-permute-start | bytes 1769480 | tf_op jit(solution)/shard_map/ppermute | solution.py:70
  205.0 6.3 collective-permute-done.42
  217.3 9.2 %collective-permute-done.37 = bf16[128,2304]{1,0:T(8,128)(2,1)S(1)} collective-permute-done((bf16[128,2304]{1,0:T(8,128)(2,1)S(1)}, bf16[128,2304]{1,0:T(8,128)(2,1)S(1)}, u32[]{:S(2)}, u32[]{:S(2)}) %collective-permute-start.37) | collective-permute-done | bytes 589856 | tf_op jit(solution)/shard_map/ppermute | solution.py:70
  227.8 11.7 %collective-permute-done.45 = bf16[288,2304]{1,0:T(8,128)(2,1)S(1)} collective-permute-done((bf16[288,2304]{1,0:T(8,128)(2,1)}, bf16[288,2304]{1,0:T(8,128)(2,1)S(1)}, u32[]{:S(2)}, u32[]{:S(2)}) %collective-permute-start.45) | collective-permute-done | bytes 1327136 | tf_op jit(solution)/shard_map/ppermute | solution.py:138
  241.1 4.6 collective-permute-start.49
  246.2 8.9 %collective-permute-done.51 = bf16[128,2304]{1,0:T(8,128)(2,1)S(1)} collective-permute-done((bf16[128,2304]{1,0:T(8,128)(2,1)S(1)}, bf16[128,2304]{1,0:T(8,128)(2,1)S(1)}, u32[]{:S(2)}, u32[]{:S(2)}) %collective-permute-start.51) | collective-permute-done | bytes 589856 | tf_op jit(solution)/shard_map/ppermute | solution.py:70
  256.5 12.1 %collective-permute-done.41 = bf16[288,2304]{1,0:T(8,128)(2,1)S(1)} collective-permute-done((bf16[288,2304]{1,0:T(8,128)(2,1)}, bf16[288,2304]{1,0:T(8,128)(2,1)S(1)}, u32[]{:S(2)}, u32[]{:S(2)}) %collective-permute-start.41) | collective-permute-done | bytes 1327136 | tf_op jit(solution)/shard_map/ppermute | solution.py:138
  270.9 12.4 %collective-permute-done.52 = bf16[128,2304]{1,0:T(8,128)(2,1)S(1)} collective-permute-done((bf16[128,2304]{1,0:T(8,128)(2,1)S(1)}, bf16[128,2304]{1,0:T(8,128)(2,1)S(1)}, u32[]{:S(2)}, u32[]{:S(2)}) %collective-permute-start.52) | collective-permute-done | bytes 589856 | tf_op jit(solution)/shard_map/ppermute | solution.py:70
  283.7 12.0 %collective-permute-done.47 = bf16[288,2304]{1,0:T(8,128)(2,1)S(1)} collective-permute-done((bf16[288,2304]{1,0:T(8,128)(2,1)S(1)}, bf16[288,2304]{1,0:T(8,128)(2,1)S(1)}, u32[]{:S(2)}, u32[]{:S(2)}) %collective-permute-start.47) | collective-permute-done | bytes 1327136 | tf_op jit(solution)/shard_map/ppermute | solution.py:138
  301.1 10.7 %collective-permute-done.58 = bf16[128,2304]{1,0:T(8,128)(2,1)S(1)} collective-permute-done((bf16[128,2304]{1,0:T(8,128)(2,1)S(1)}, bf16[128,2304]{1,0:T(8,128)(2,1)S(1)}, u32[]{:S(2)}, u32[]{:S(2)}) %collective-permute-start.58) | collective-permute-done | bytes 589856 | tf_op jit(solution)/shard_map/ppermute | solution.py:70
  335.6 8.2 %collective-permute-done.61 = bf16[128,2304]{1,0:T(8,128)(2,1)S(1)} collective-permute-done((bf16[128,2304]{1,0:T(8,128)(2,1)S(1)}, bf16[128,2304]{1,0:T(8,128)(2,1)S(1)}, u32[]{:S(2)}, u32[]{:S(2)}) %collective-permute-start.61) | collective-permute-done | bytes 589856 | tf_op jit(solution)/shard_map/ppermute | solution.py:70
  344.3 4.4 collective-permute-start.62
  356.2 4.8 collective-permute-done.62
  362.4 7.2 collective-permute-start.63
  375.3 5.3 collective-permute-done.63
  380.6 5.0 collective-permute-done.66
  392.5 4.8 collective-permute-start.69
  399.1 9.1 %collective-permute-done.71 = bf16[128,2304]{1,0:T(8,128)(2,1)S(1)} collective-permute-done((bf16[128,2304]{1,0:T(8,128)(2,1)S(1)}, bf16[128,2304]{1,0:T(8,128)(2,1)S(1)}, u32[]{:S(2)}, u32[]{:S(2)}) %collective-permute-start.71) | collective-permute-done | bytes 589856 | tf_op jit(solution)/shard_map/ppermute | solution.py:70
  416.3 4.3 convolution_add_fusion.3
  422.8 9.8 %collective-permute-done.72 = bf16[128,2304]{1,0:T(8,128)(2,1)S(1)} collective-permute-done((bf16[128,2304]{1,0:T(8,128)(2,1)S(1)}, bf16[128,2304]{1,0:T(8,128)(2,1)S(1)}, u32[]{:S(2)}, u32[]{:S(2)}) %collective-permute-start.72) | collective-permute-done | bytes 589856 | tf_op jit(solution)/shard_map/ppermute | solution.py:70
  440.1 4.3 convolution_add_fusion.1
  446.0 9.9 %collective-permute-done.78 = bf16[128,2304]{1,0:T(8,128)(2,1)S(1)} collective-permute-done((bf16[128,2304]{1,0:T(8,128)(2,1)S(1)}, bf16[128,2304]{1,0:T(8,128)(2,1)S(1)}, u32[]{:S(2)}, u32[]{:S(2)}) %collective-permute-start.78) | collective-permute-done | bytes 589856 | tf_op jit(solution)/shard_map/ppermute | solution.py:70
  457.1 3.5 fusion.26
  462.3 4.5 convolution_add_fusion.2
  469.9 4.4 fusion.148
  480.6 8.5 %convolution_convert_fusion = bf16[1152,2304]{1,0:T(8,128)(2,1)S(1)} fusion(bf16[1024,1152]{1,0:T(8,128)(2,1)S(1)} %pad_maximum_fusion.1, bf16[1024,2304]{1,0:T(8,128)(2,1)} %constant_dynamic-update-slice_fusion.12), kind=kOutput, calls=%fused_computation | convolution fusion | flops 5438472192 | bytes 12386304 | tf_op jit(solution)/shard_map/dot_general | solution.py:51
  493.1 4.4 collective-permute-start.83
  498.3 8.5 %convolution_convert_fusion.2 = bf16[1152,2304]{1,0:T(8,128)(2,1)S(1)} fusion(bf16[1024,1152]{1,0:T(8,128)(2,1)S(1)} %pad_maximum_fusion.2, bf16[1024,2304]{1,0:T(8,128)(2,1)} %constant_dynamic-update-slice_fusion.20), kind=kOutput, calls=%fused_computation.2 | convolution fusion | flops 5438472192 | bytes 12386304 | tf_op jit(solution)/shard_map/dot_general | solution.py:51
  512.5 9.2 %collective-permute-start.85 = (bf16[128,2304]{1,0:T(8,128)(2,1)}, bf16[128,2304]{1,0:T(8,128)(2,1)S(1)}, u32[]{:S(2)}, u32[]{:S(2)}) collective-permute-start(bf16[128,2304]{1,0:T(8,128)(2,1)} %get-tuple-element.35), channel_id=1, source_target_pairs={{0,2},{1,3},{2,4},{3,5},{4,6},{5,7},{8,10},{9,11},{10,12},{11,13},... | collective-permute-start | bytes 1769480 | tf_op jit(solution)/shard_map/ppermute | solution.py:70
  521.7 8.5 %convolution_convert_fusion.1 = bf16[1152,2304]{1,0:T(8,128)(2,1)S(1)} fusion(bf16[1024,1152]{1,0:T(8,128)(2,1)S(1)} %pad_maximum_fusion.3, bf16[1024,2304]{1,0:T(8,128)(2,1)} %constant_dynamic-update-slice_fusion.20), kind=kOutput, calls=%fused_computation.1 | convolution fusion | flops 5438472192 | bytes 12386304 | tf_op jit(solution)/shard_map/dot_general | solution.py:51
  530.5 18.4 %collective-permute-done.122 = bf16[288,2304]{1,0:T(8,128)(2,1)S(1)} collective-permute-done((bf16[288,2304]{1,0:T(8,128)(2,1)S(1)}, bf16[288,2304]{1,0:T(8,128)(2,1)S(1)}, u32[]{:S(2)}, u32[]{:S(2)}) %collective-permute-start.122) | collective-permute-done | bytes 1327136 | tf_op jit(solution)/shard_map/ppermute | solution.py:138
  550.5 14.6 %collective-permute-done.86 = bf16[128,2304]{1,0:T(8,128)(2,1)S(1)} collective-permute-done((bf16[128,2304]{1,0:T(8,128)(2,1)S(1)}, bf16[128,2304]{1,0:T(8,128)(2,1)S(1)}, u32[]{:S(2)}, u32[]{:S(2)}) %collective-permute-start.86) | collective-permute-done | bytes 589856 | tf_op jit(solution)/shard_map/ppermute | solution.py:70
  569.5 3.8 collective-permute-start.124
  579.6 7.3 collective-permute-done.119
  594.4 13.7 %collective-permute-done.116 = bf16[160,2304]{1,0:T(8,128)(2,1)S(1)} collective-permute-done((bf16[160,2304]{1,0:T(8,128)(2,1)S(1)}, bf16[160,2304]{1,0:T(8,128)(2,1)S(1)}, u32[]{:S(2)}, u32[]{:S(2)}) %collective-permute-start.116) | collective-permute-done | bytes 737312 | tf_op jit(solution)/shard_map/ppermute | solution.py:138
  608.5 25.5 %collective-permute-done.118 = bf16[128,2304]{1,0:T(8,128)(2,1)S(1)} collective-permute-done((bf16[128,2304]{1,0:T(8,128)(2,1)S(1)}, bf16[128,2304]{1,0:T(8,128)(2,1)S(1)}, u32[]{:S(2)}, u32[]{:S(2)}) %collective-permute-start.118) | collective-permute-done | bytes 589856 | tf_op jit(solution)/shard_map/ppermute | solution.py:138
  635.3 4.6 collective-permute-start.87
  640.2 9.7 %collective-permute-done.88 = bf16[128,2304]{1,0:T(8,128)(2,1)S(1)} collective-permute-done((bf16[128,2304]{1,0:T(8,128)(2,1)S(1)}, bf16[128,2304]{1,0:T(8,128)(2,1)S(1)}, u32[]{:S(2)}, u32[]{:S(2)}) %collective-permute-start.88) | collective-permute-done | bytes 589856 | tf_op jit(solution)/shard_map/ppermute | solution.py:70
  651.4 11.0 %collective-permute-done.123 = bf16[288,2304]{1,0:T(8,128)(2,1)S(1)} collective-permute-done((bf16[288,2304]{1,0:T(8,128)(2,1)S(1)}, bf16[288,2304]{1,0:T(8,128)(2,1)S(1)}, u32[]{:S(2)}, u32[]{:S(2)}) %collective-permute-start.123) | collective-permute-done | bytes 1327136 | tf_op jit(solution)/shard_map/ppermute | solution.py:138
  667.2 5.9 collective-permute-done.117
  683.2 3.2 multiply_convert_fusion
  700.8 7.4 collective-permute-done.94
  712.9 5.4 collective-permute-done.110
  718.3 3.5 collective-permute-start.96
  725.5 7.4 collective-permute-done.96
  733.9 18.9 %collective-permute-start.97 = (bf16[128,2304]{1,0:T(8,128)(2,1)S(1)}, bf16[128,2304]{1,0:T(8,128)(2,1)S(1)}, u32[]{:S(2)}, u32[]{:S(2)}) collective-permute-start(bf16[128,2304]{1,0:T(8,128)(2,1)S(1)} %get-tuple-element.101), channel_id=1, source_target_pairs={{0,2},{1,3},{2,4},{3,5},{4,6},{5,7},{8,10},{9,11},{10,12},{11,13},... | collective-permute-start | bytes 1769480 | tf_op jit(solution)/shard_map/ppermute | solution.py:70
  764.7 5.9 collective-permute-done.99
  772.4 11.9 %collective-permute-done.103 = bf16[4,72,1024]{2,1,0:T(8,128)(2,1)S(1)} collective-permute-done((bf16[4,72,1024]{2,1,0:T(8,128)(2,1)S(1)}, bf16[4,72,1024]{2,1,0:T(8,128)(2,1)S(1)}, u32[]{:S(2)}, u32[]{:S(2)}) %collective-permute-start.103) | collective-permute-done | bytes 589856 | tf_op jit(solution)/shard_map/ppermute | solution.py:138
  786.6 14.5 %collective-permute-start.104 = (bf16[72,1024]{1,0:T(8,128)(2,1)S(1)}, bf16[72,1024]{1,0:T(8,128)(2,1)S(1)}, u32[]{:S(2)}, u32[]{:S(2)}) collective-permute-start(bf16[72,1024]{1,0:T(8,128)(2,1)S(1)} %get-tuple-element.133), channel_id=1, source_target_pairs={{2,0},{3,1},{4,2},{5,3},{6,4},{7,5},{0,6},{1,7},{10,8},{11,9},{12,... | collective-permute-start | bytes 442376 | tf_op jit(solution)/shard_map/ppermute | solution.py:125
  805.5 9.9 %collective-permute-done.105 = bf16[72,1024]{1,0:T(8,128)(2,1)S(1)} collective-permute-done((bf16[72,1024]{1,0:T(8,128)(2,1)S(1)}, bf16[72,1024]{1,0:T(8,128)(2,1)S(1)}, u32[]{:S(2)}, u32[]{:S(2)}) %collective-permute-start.105) | collective-permute-done | bytes 147488 | tf_op jit(solution)/shard_map/ppermute | solution.py:125
  (645 shorter events, 264.9 us)
Async XLA Ops:
  1.4 17.5 %collective-permute-start.2 = (bf16[4,32,72]{2,0,1:T(4,128)(2,1)S(1)}, bf16[4,32,72]{2,0,1:T(4,128)(2,1)S(1)}, u32[]{:S(2)}, u32[]{:S(2)}) collective-permute-start(bf16[4,32,72]{2,0,1:T(4,128)(2,1)S(1)} %constant_dynamic-update-slice_fusion.29), channel_id=1, source_target_pairs={{0,24},{8,16},{16,8},{24,0},{1,25},{9,17},{17,9},{25,1},{2,26},{10... | collective-permute-start | bytes 55304 | tf_op jit(solution)/shard_map/ppermute | solution.py:138
  6.0 52.3 %collective-permute-start.24 = (bf16[64,2304]{1,0:T(8,128)(2,1)}, bf16[64,2304]{1,0:T(8,128)(2,1)}, u32[]{:S(2)}, u32[]{:S(2)}) collective-permute-start(bf16[64,2304]{1,0:T(8,128)(2,1)} %param.26), channel_id=1, source_target_pairs={{0,0},{4,1},{8,2},{12,3},{16,4},{20,5},{24,6},{28,7},{1,8},{5,9},{... | collective-permute-start | bytes 884744 | tf_op jit(solution)/shard_map/ppermute | solution.py:296
  15.3 31.7 %collective-permute-start.7 = (bf16[72,1024]{1,0:T(8,128)(2,1)S(1)}, bf16[72,1024]{1,0:T(8,128)(2,1)S(1)}, u32[]{:S(2)}, u32[]{:S(2)}) collective-permute-start(bf16[72,1024]{1,0:T(8,128)(2,1)S(1)} %bitcast.271), channel_id=1, source_target_pairs={{2,0},{3,1},{4,2},{5,3},{6,4},{7,5},{0,6},{1,7},{10,8},{11,9},{12,... | collective-permute-start | bytes 442376 | tf_op jit(solution)/shard_map/ppermute | solution.py:125
  20.0 22.5 %collective-permute-start.3 = (bf16[4,32,72]{2,0,1:T(4,128)(2,1)S(1)}, bf16[4,32,72]{2,0,1:T(4,128)(2,1)S(1)}, u32[]{:S(2)}, u32[]{:S(2)}) collective-permute-start(bf16[4,32,72]{2,0,1:T(4,128)(2,1)S(1)} %bitcast.280), channel_id=1, source_target_pairs={{2,0},{3,1},{4,2},{5,3},{6,4},{7,5},{0,6},{1,7},{10,8},{11,9},{12,... | collective-permute-start | bytes 55304 | tf_op jit(solution)/shard_map/ppermute | solution.py:125
  25.0 27.6 %collective-permute-start.8 = (bf16[72,1024]{1,0:T(8,128)(2,1)S(1)}, bf16[72,1024]{1,0:T(8,128)(2,1)S(1)}, u32[]{:S(2)}, u32[]{:S(2)}) collective-permute-start(bf16[72,1024]{1,0:T(8,128)(2,1)S(1)} %bitcast.273), channel_id=1, source_target_pairs={{4,0},{5,1},{6,2},{7,3},{0,4},{1,5},{2,6},{3,7},{12,8},{13,9},{14,... | collective-permute-start | bytes 442376 | tf_op jit(solution)/shard_map/ppermute | solution.py:125
  33.9 19.0 %collective-permute-start.9 = (bf16[72,1024]{1,0:T(8,128)(2,1)S(1)}, bf16[72,1024]{1,0:T(8,128)(2,1)S(1)}, u32[]{:S(2)}, u32[]{:S(2)}) collective-permute-start(bf16[72,1024]{1,0:T(8,128)(2,1)S(1)} %bitcast.272), channel_id=1, source_target_pairs={{6,0},{7,1},{0,2},{1,3},{2,4},{3,5},{4,6},{5,7},{14,8},{15,9},{8,1... | collective-permute-start | bytes 442376 | tf_op jit(solution)/shard_map/ppermute | solution.py:125
  45.7 49.6 %collective-permute-start.18 = (bf16[128,2304]{1,0:T(8,128)(2,1)}, bf16[128,2304]{1,0:T(8,128)(2,1)}, u32[]{:S(2)}, u32[]{:S(2)}) collective-permute-start(bf16[128,2304]{1,0:T(8,128)(2,1)} %multiply_convert_fusion.12), channel_id=1, source_target_pairs={{2,0},{3,1},{4,2},{5,3},{6,4},{7,5},{10,8},{11,9},{12,10},{13,11},... | collective-permute-start | bytes 1769480 | tf_op jit(solution)/shard_map/ppermute | solution.py:70
  47.0 51.2 %collective-permute-start.17 = (bf16[128,2304]{1,0:T(8,128)(2,1)}, bf16[128,2304]{1,0:T(8,128)(2,1)}, u32[]{:S(2)}, u32[]{:S(2)}) collective-permute-start(bf16[128,2304]{1,0:T(8,128)(2,1)} %multiply_convert_fusion.12), channel_id=1, source_target_pairs={{0,2},{1,3},{2,4},{3,5},{4,6},{5,7},{8,10},{9,11},{10,12},{11,13},... | collective-permute-start | bytes 1769480 | tf_op jit(solution)/shard_map/ppermute | solution.py:70
  57.3 21.8 %collective-permute-start.11 = (bf16[4,72,1024]{2,0,1:T(4,128)(2,1)S(1)}, bf16[4,72,1024]{2,0,1:T(4,128)(2,1)S(1)}, u32[]{:S(2)}, u32[]{:S(2)}) collective-permute-start(bf16[4,72,1024]{2,0,1:T(4,128)(2,1)S(1)} %constant_dynamic-slice_fusion.2), channel_id=1, source_target_pairs={{0,8},{8,0},{16,24},{24,16},{1,9},{9,1},{17,25},{25,17},{2,10},{10... | collective-permute-start | bytes 1769480 | tf_op jit(solution)/shard_map/ppermute | solution.py:138
  57.4 21.4 %collective-permute-start.10 = (bf16[4,72,1024]{2,0,1:T(4,128)(2,1)S(1)}, bf16[4,72,1024]{2,0,1:T(4,128)(2,1)S(1)}, u32[]{:S(2)}, u32[]{:S(2)}) collective-permute-start(bf16[4,72,1024]{2,0,1:T(4,128)(2,1)S(1)} %constant_dynamic-slice_fusion.2), channel_id=1, source_target_pairs={{0,1},{1,0},{2,3},{3,2},{4,5},{5,4},{6,7},{7,6},{8,9},{9,8},{10,11... | collective-permute-start | bytes 1769480 | tf_op jit(solution)/shard_map/ppermute | solution.py:73
  60.3 18.5 %collective-permute-start.26 = (bf16[64,2304]{1,0:T(8,128)(2,1)}, bf16[64,2304]{1,0:T(8,128)(2,1)S(1)}, u32[]{:S(2)}, u32[]{:S(2)}) collective-permute-start(bf16[64,2304]{1,0:T(8,128)(2,1)} %collective-permute-done.24), channel_id=1, source_target_pairs={{0,8},{8,0},{16,24},{24,16},{1,9},{9,1},{17,25},{25,17},{2,10},{10... | collective-permute-start | bytes 884744 | tf_op jit(solution)/shard_map/ppermute | solution.py:138
  79.1 39.3 %collective-permute-start.13 = (bf16[4,72,1024]{2,0,1:T(4,128)(2,1)S(1)}, bf16[4,72,1024]{2,0,1:T(4,128)(2,1)S(1)}, u32[]{:S(2)}, u32[]{:S(2)}) collective-permute-start(bf16[4,72,1024]{2,0,1:T(4,128)(2,1)S(1)} %constant_dynamic-slice_fusion.2), channel_id=1, source_target_pairs={{0,16},{8,24},{16,0},{24,8},{1,17},{9,25},{17,1},{25,9},{2,18},{10... | collective-permute-start | bytes 1769480 | tf_op jit(solution)/shard_map/ppermute | solution.py:138
  95.2 23.3 %collective-permute-start.15 = (bf16[4,72,1024]{2,0,1:T(4,128)(2,1)S(1)}, bf16[4,72,1024]{2,0,1:T(4,128)(2,1)S(1)}, u32[]{:S(2)}, u32[]{:S(2)}) collective-permute-start(bf16[4,72,1024]{2,0,1:T(4,128)(2,1)S(1)} %constant_dynamic-slice_fusion.2), channel_id=1, source_target_pairs={{0,24},{8,16},{16,8},{24,0},{1,25},{9,17},{17,9},{25,1},{2,26},{10... | collective-permute-start | bytes 1769480 | tf_op jit(solution)/shard_map/ppermute | solution.py:138
  95.3 17.1 %collective-permute-start.30 = (bf16[64,2304]{1,0:T(8,128)(2,1)}, bf16[64,2304]{1,0:T(8,128)(2,1)S(1)}, u32[]{:S(2)}, u32[]{:S(2)}) collective-permute-start(bf16[64,2304]{1,0:T(8,128)(2,1)} %collective-permute-done.24), channel_id=1, source_target_pairs={{0,24},{8,16},{16,8},{24,0},{1,25},{9,17},{17,9},{25,1},{2,26},{10... | collective-permute-start | bytes 884744 | tf_op jit(solution)/shard_map/ppermute | solution.py:138
  98.2 20.8 %collective-permute-start.20 = (bf16[128,2304]{1,0:T(8,128)(2,1)}, bf16[128,2304]{1,0:T(8,128)(2,1)S(1)}, u32[]{:S(2)}, u32[]{:S(2)}) collective-permute-start(bf16[128,2304]{1,0:T(8,128)(2,1)} %collective-permute-done.18), channel_id=1, source_target_pairs={{2,0},{3,1},{4,2},{5,3},{10,8},{11,9},{12,10},{13,11},{18,16},{19,... | collective-permute-start | bytes 1769480 | tf_op jit(solution)/shard_map/ppermute | solution.py:70
  99.5 19.6 %collective-permute-start.19 = (bf16[128,2304]{1,0:T(8,128)(2,1)}, bf16[128,2304]{1,0:T(8,128)(2,1)S(1)}, u32[]{:S(2)}, u32[]{:S(2)}) collective-permute-start(bf16[128,2304]{1,0:T(8,128)(2,1)} %collective-permute-done.17), channel_id=1, source_target_pairs={{2,4},{3,5},{4,6},{5,7},{10,12},{11,13},{12,14},{13,15},{18,20},{1... | collective-permute-start | bytes 1769480 | tf_op jit(solution)/shard_map/ppermute | solution.py:70
  118.5 22.7 %collective-permute-start.31 = (bf16[64,2304]{1,0:T(8,128)(2,1)S(1)}, bf16[64,2304]{1,0:T(8,128)(2,1)S(1)}, u32[]{:S(2)}, u32[]{:S(2)}) collective-permute-start(bf16[64,2304]{1,0:T(8,128)(2,1)S(1)} %collective-permute-done.30), channel_id=1, source_target_pairs={{0,1},{1,0},{2,3},{3,2},{4,5},{5,4},{6,7},{7,6},{8,9},{9,8},{10,11... | collective-permute-start | bytes 884744 | tf_op jit(solution)/shard_map/ppermute | solution.py:73
  119.2 17.5 %collective-permute-start.22 = (bf16[128,2304]{1,0:T(8,128)(2,1)S(1)}, bf16[128,2304]{1,0:T(8,128)(2,1)S(1)}, u32[]{:S(2)}, u32[]{:S(2)}) collective-permute-start(bf16[128,2304]{1,0:T(8,128)(2,1)S(1)} %collective-permute-done.20), channel_id=1, source_target_pairs={{2,0},{3,1},{10,8},{11,9},{18,16},{19,17},{26,24},{27,25}} | collective-permute-start | bytes 1769480 | tf_op jit(solution)/shard_map/ppermute | solution.py:70
  150.6 34.3 %collective-permute-start.39 = (bf16[288,2304]{1,0:T(8,128)(2,1)S(1)}, bf16[288,2304]{1,0:T(8,128)(2,1)}, u32[]{:S(2)}, u32[]{:S(2)}) collective-permute-start(bf16[288,2304]{1,0:T(8,128)(2,1)S(1)} %copy-done.17), channel_id=1, source_target_pairs={{0,8},{8,0},{16,24},{24,16},{1,9},{9,1},{17,25},{25,17},{2,10},{10... | collective-permute-start | bytes 3981320 | tf_op jit(solution)/shard_map/ppermute | solution.py:138
  151.3 37.0 %collective-permute-start.40 = (bf16[288,2304]{1,0:T(8,128)(2,1)S(1)}, bf16[288,2304]{1,0:T(8,128)(2,1)}, u32[]{:S(2)}, u32[]{:S(2)}) collective-permute-start(bf16[288,2304]{1,0:T(8,128)(2,1)S(1)} %copy-done.17), channel_id=1, source_target_pairs={{0,16},{8,24},{16,0},{24,8},{1,17},{9,25},{17,1},{25,9},{2,18},{10... | collective-permute-start | bytes 3981320 | tf_op jit(solution)/shard_map/ppermute | solution.py:138
  151.6 59.7 %collective-permute-start.42 = (bf16[288,2304]{1,0:T(8,128)(2,1)}, bf16[288,2304]{1,0:T(8,128)(2,1)}, u32[]{:S(2)}, u32[]{:S(2)}) collective-permute-start(bf16[288,2304]{1,0:T(8,128)(2,1)} %param.28), channel_id=1, source_target_pairs={{0,8},{8,0},{16,24},{24,16},{1,9},{9,1},{17,25},{25,17},{2,10},{10... | collective-permute-start | bytes 3981320 | tf_op jit(solution)/shard_map/ppermute | solution.py:138
  154.2 20.4 %collective-permute-start.35 = (bf16[128,2304]{1,0:T(8,128)(2,1)}, bf16[128,2304]{1,0:T(8,128)(2,1)S(1)}, u32[]{:S(2)}, u32[]{:S(2)}) collective-permute-start(bf16[128,2304]{1,0:T(8,128)(2,1)} %slice.546), channel_id=1, source_target_pairs={{6,4},{7,5},{14,12},{15,13},{22,20},{23,21},{30,28},{31,29}} | collective-permute-start | bytes 1769480 | tf_op jit(solution)/shard_map/ppermute | solution.py:70
  164.9 17.0 %collective-permute-start.33 = (bf16[128,2304]{1,0:T(8,128)(2,1)}, bf16[128,2304]{1,0:T(8,128)(2,1)}, u32[]{:S(2)}, u32[]{:S(2)}) collective-permute-start(bf16[128,2304]{1,0:T(8,128)(2,1)} %add_convert_fusion.20), channel_id=1, source_target_pairs={{0,2},{1,3},{2,4},{3,5},{8,10},{9,11},{10,12},{11,13},{16,18},{17,... | collective-permute-start | bytes 1769480 | tf_op jit(solution)/shard_map/ppermute | solution.py:70
  174.6 40.6 %collective-permute-start.43 = (bf16[288,2304]{1,0:T(8,128)(2,1)}, bf16[288,2304]{1,0:T(8,128)(2,1)S(1)}, u32[]{:S(2)}, u32[]{:S(2)}) collective-permute-start(bf16[288,2304]{1,0:T(8,128)(2,1)} %param.28), channel_id=1, source_target_pairs={{0,16},{8,24},{16,0},{24,8},{1,17},{9,25},{17,1},{25,9},{2,18},{10... | collective-permute-start | bytes 3981320 | tf_op jit(solution)/shard_map/ppermute | solution.py:138
  181.9 57.7 %collective-permute-start.45 = (bf16[288,2304]{1,0:T(8,128)(2,1)}, bf16[288,2304]{1,0:T(8,128)(2,1)S(1)}, u32[]{:S(2)}, u32[]{:S(2)}) collective-permute-start(bf16[288,2304]{1,0:T(8,128)(2,1)} %param.29), channel_id=1, source_target_pairs={{0,8},{8,0},{16,24},{24,16},{1,9},{9,1},{17,25},{25,17},{2,10},{10... | collective-permute-start | bytes 3981320 | tf_op jit(solution)/shard_map/ppermute | solution.py:138
  188.3 52.9 %collective-permute-start.46 = (bf16[288,2304]{1,0:T(8,128)(2,1)S(1)}, bf16[288,2304]{1,0:T(8,128)(2,1)S(1)}, u32[]{:S(2)}, u32[]{:S(2)}) collective-permute-start(bf16[288,2304]{1,0:T(8,128)(2,1)S(1)} %copy-done.19), channel_id=1, source_target_pairs={{0,16},{8,24},{16,0},{24,8},{1,17},{9,25},{17,1},{25,9},{2,18},{10... | collective-permute-start | bytes 3981320 | tf_op jit(solution)/shard_map/ppermute | solution.py:138
  191.1 25.6 %collective-permute-start.34 = (bf16[128,2304]{1,0:T(8,128)(2,1)S(1)}, bf16[128,2304]{1,0:T(8,128)(2,1)S(1)}, u32[]{:S(2)}, u32[]{:S(2)}) collective-permute-start(bf16[128,2304]{1,0:T(8,128)(2,1)S(1)} %get-tuple-element.105), channel_id=1, source_target_pairs={{0,2},{1,3},{2,4},{3,5},{4,6},{5,7},{8,10},{9,11},{10,12},{11,13},... | collective-permute-start | bytes 1769480 | tf_op jit(solution)/shard_map/ppermute | solution.py:70
  215.2 53.4 %collective-permute-start.41 = (bf16[288,2304]{1,0:T(8,128)(2,1)}, bf16[288,2304]{1,0:T(8,128)(2,1)S(1)}, u32[]{:S(2)}, u32[]{:S(2)}) collective-permute-start(bf16[288,2304]{1,0:T(8,128)(2,1)} %collective-permute-done.39), channel_id=1, source_target_pairs={{0,16},{8,24},{16,0},{24,8},{1,17},{9,25},{17,1},{25,9},{2,18},{10... | collective-permute-start | bytes 3981320 | tf_op jit(solution)/shard_map/ppermute | solution.py:138
  216.7 54.0 %collective-permute-start.44 = (bf16[288,2304]{1,0:T(8,128)(2,1)S(1)}, bf16[288,2304]{1,0:T(8,128)(2,1)S(1)}, u32[]{:S(2)}, u32[]{:S(2)}) collective-permute-start(bf16[288,2304]{1,0:T(8,128)(2,1)S(1)} %collective-permute-done.43), channel_id=1, source_target_pairs={{0,8},{8,0},{16,24},{24,16},{1,9},{9,1},{17,25},{25,17},{2,10},{10... | collective-permute-start | bytes 3981320 | tf_op jit(solution)/shard_map/ppermute | solution.py:138
  227.8 18.1 %collective-permute-start.38 = (bf16[128,2304]{1,0:T(8,128)(2,1)S(1)}, bf16[128,2304]{1,0:T(8,128)(2,1)S(1)}, u32[]{:S(2)}, u32[]{:S(2)}) collective-permute-start(bf16[128,2304]{1,0:T(8,128)(2,1)S(1)} %get-tuple-element.70), channel_id=1, source_target_pairs={{0,1},{1,0},{2,3},{3,2},{4,5},{5,4},{6,7},{7,6},{8,9},{9,8},{10,11... | collective-permute-start | bytes 1769480 | tf_op jit(solution)/shard_map/ppermute | solution.py:73
  245.8 49.9 %collective-permute-start.47 = (bf16[288,2304]{1,0:T(8,128)(2,1)S(1)}, bf16[288,2304]{1,0:T(8,128)(2,1)S(1)}, u32[]{:S(2)}, u32[]{:S(2)}) collective-permute-start(bf16[288,2304]{1,0:T(8,128)(2,1)S(1)} %collective-permute-done.45), channel_id=1, source_target_pairs={{0,16},{8,24},{16,0},{24,8},{1,17},{9,25},{17,1},{25,9},{2,18},{10... | collective-permute-start | bytes 3981320 | tf_op jit(solution)/shard_map/ppermute | solution.py:138
  283.7 17.3 %collective-permute-start.53 = (bf16[128,2304]{1,0:T(8,128)(2,1)S(1)}, bf16[128,2304]{1,0:T(8,128)(2,1)S(1)}, u32[]{:S(2)}, u32[]{:S(2)}) collective-permute-start(bf16[128,2304]{1,0:T(8,128)(2,1)S(1)} %get-tuple-element.66), channel_id=1, source_target_pairs={{0,1},{1,0},{2,3},{3,2},{4,5},{5,4},{6,7},{7,6},{8,9},{9,8},{10,11... | collective-permute-start | bytes 1769480 | tf_op jit(solution)/shard_map/ppermute | solution.py:73
  335.4 20.8 %collective-permute-start.56 = (bf16[128,2304]{1,0:T(8,128)(2,1)S(1)}, bf16[128,2304]{1,0:T(8,128)(2,1)S(1)}, u32[]{:S(2)}, u32[]{:S(2)}) collective-permute-start(bf16[128,2304]{1,0:T(8,128)(2,1)S(1)} %slice.542), channel_id=1, source_target_pairs={{0,1},{1,0},{2,3},{3,2},{4,5},{5,4},{6,7},{7,6},{8,9},{9,8},{10,11... | collective-permute-start | bytes 1769480 | tf_op jit(solution)/shard_map/ppermute | solution.py:73
  344.3 16.7 %collective-permute-start.62 = (bf16[128,2304]{1,0:T(8,128)(2,1)S(1)}, bf16[128,2304]{1,0:T(8,128)(2,1)S(1)}, u32[]{:S(2)}, u32[]{:S(2)}) collective-permute-start(bf16[128,2304]{1,0:T(8,128)(2,1)S(1)} %get-tuple-element.91), channel_id=1, source_target_pairs={{0,2},{1,3},{2,4},{3,5},{8,10},{9,11},{10,12},{11,13},{16,18},{17,... | collective-permute-start | bytes 1769480 | tf_op jit(solution)/shard_map/ppermute | solution.py:70
  356.2 19.1 %collective-permute-start.48 = (bf16[128,2304]{1,0:T(8,128)(2,1)}, bf16[128,2304]{1,0:T(8,128)(2,1)}, u32[]{:S(2)}, u32[]{:S(2)}) collective-permute-start(bf16[128,2304]{1,0:T(8,128)(2,1)} %slice.544), channel_id=1, source_target_pairs={{0,1},{1,0},{2,3},{3,2},{4,5},{5,4},{6,7},{7,6},{8,9},{9,8},{10,11... | collective-permute-start | bytes 1769480 | tf_op jit(solution)/shard_map/ppermute | solution.py:73
  362.4 18.1 %collective-permute-start.63 = (bf16[128,2304]{1,0:T(8,128)(2,1)}, bf16[128,2304]{1,0:T(8,128)(2,1)}, u32[]{:S(2)}, u32[]{:S(2)}) collective-permute-start(bf16[128,2304]{1,0:T(8,128)(2,1)} %get-tuple-element.89), channel_id=1, source_target_pairs={{0,2},{1,3},{2,4},{3,5},{4,6},{5,7},{8,10},{9,11},{10,12},{11,13},... | collective-permute-start | bytes 1769480 | tf_op jit(solution)/shard_map/ppermute | solution.py:70
  390.9 17.3 %collective-permute-start.71 = (bf16[128,2304]{1,0:T(8,128)(2,1)S(1)}, bf16[128,2304]{1,0:T(8,128)(2,1)S(1)}, u32[]{:S(2)}, u32[]{:S(2)}) collective-permute-start(bf16[128,2304]{1,0:T(8,128)(2,1)S(1)} %get-tuple-element.78), channel_id=1, source_target_pairs={{2,0},{3,1},{4,2},{5,3},{6,4},{7,5},{10,8},{11,9},{12,10},{13,11},... | collective-permute-start | bytes 1769480 | tf_op jit(solution)/shard_map/ppermute | solution.py:70
  392.5 16.9 %collective-permute-start.69 = (bf16[128,2304]{1,0:T(8,128)(2,1)S(1)}, bf16[128,2304]{1,0:T(8,128)(2,1)S(1)}, u32[]{:S(2)}, u32[]{:S(2)}) collective-permute-start(bf16[128,2304]{1,0:T(8,128)(2,1)S(1)} %get-tuple-element.78), channel_id=1, source_target_pairs={{0,2},{1,3},{2,4},{3,5},{4,6},{5,7},{8,10},{9,11},{10,12},{11,13},... | collective-permute-start | bytes 1769480 | tf_op jit(solution)/shard_map/ppermute | solution.py:70
  414.3 18.4 %collective-permute-start.72 = (bf16[128,2304]{1,0:T(8,128)(2,1)S(1)}, bf16[128,2304]{1,0:T(8,128)(2,1)S(1)}, u32[]{:S(2)}, u32[]{:S(2)}) collective-permute-start(bf16[128,2304]{1,0:T(8,128)(2,1)S(1)} %collective-permute-done.71), channel_id=1, source_target_pairs={{2,0},{3,1},{4,2},{5,3},{10,8},{11,9},{12,10},{13,11},{18,16},{19,... | collective-permute-start | bytes 1769480 | tf_op jit(solution)/shard_map/ppermute | solution.py:70
  415.6 17.1 %collective-permute-start.70 = (bf16[128,2304]{1,0:T(8,128)(2,1)S(1)}, bf16[128,2304]{1,0:T(8,128)(2,1)S(1)}, u32[]{:S(2)}, u32[]{:S(2)}) collective-permute-start(bf16[128,2304]{1,0:T(8,128)(2,1)S(1)} %collective-permute-done.69), channel_id=1, source_target_pairs={{2,4},{3,5},{4,6},{5,7},{10,12},{11,13},{12,14},{13,15},{18,20},{1... | collective-permute-start | bytes 1769480 | tf_op jit(solution)/shard_map/ppermute | solution.py:70
  421.5 129.0 %collective-permute-start.68 = (bf16[128,2304]{1,0:T(8,128)(2,1)}, bf16[128,2304]{1,0:T(8,128)(2,1)S(1)}, u32[]{:S(2)}, u32[]{:S(2)}) collective-permute-start(bf16[128,2304]{1,0:T(8,128)(2,1)} %slice.540), channel_id=1, source_target_pairs={{0,1},{1,0},{2,3},{3,2},{4,5},{5,4},{6,7},{7,6},{8,9},{9,8},{10,11... | collective-permute-start | bytes 1769480 | tf_op jit(solution)/shard_map/ppermute | solution.py:73
  437.7 18.2 %collective-permute-start.78 = (bf16[128,2304]{1,0:T(8,128)(2,1)S(1)}, bf16[128,2304]{1,0:T(8,128)(2,1)S(1)}, u32[]{:S(2)}, u32[]{:S(2)}) collective-permute-start(bf16[128,2304]{1,0:T(8,128)(2,1)S(1)} %collective-permute-done.72), channel_id=1, source_target_pairs={{2,0},{3,1},{10,8},{11,9},{18,16},{19,17},{26,24},{27,25}} | collective-permute-start | bytes 1769480 | tf_op jit(solution)/shard_map/ppermute | solution.py:70
  439.0 16.9 %collective-permute-start.77 = (bf16[128,2304]{1,0:T(8,128)(2,1)S(1)}, bf16[128,2304]{1,0:T(8,128)(2,1)S(1)}, u32[]{:S(2)}, u32[]{:S(2)}) collective-permute-start(bf16[128,2304]{1,0:T(8,128)(2,1)S(1)} %collective-permute-done.70), channel_id=1, source_target_pairs={{4,6},{5,7},{12,14},{13,15},{20,22},{21,23},{28,30},{29,31}} | collective-permute-start | bytes 1769480 | tf_op jit(solution)/shard_map/ppermute | solution.py:70
  444.5 62.5 %collective-permute-start.76 = (bf16[128,2304]{1,0:T(8,128)(2,1)S(1)}, bf16[128,2304]{1,0:T(8,128)(2,1)S(1)}, u32[]{:S(2)}, u32[]{:S(2)}) collective-permute-start(bf16[128,2304]{1,0:T(8,128)(2,1)S(1)} %slice.538), channel_id=1, source_target_pairs={{0,1},{1,0},{2,3},{3,2},{4,5},{5,4},{6,7},{7,6},{8,9},{9,8},{10,11... | collective-permute-start | bytes 1769480 | tf_op jit(solution)/shard_map/ppermute | solution.py:73
  466.9 22.5 %collective-permute-start.74 = (bf16[128,2304]{1,0:T(8,128)(2,1)S(1)}, bf16[128,2304]{1,0:T(8,128)(2,1)S(1)}, u32[]{:S(2)}, u32[]{:S(2)}) collective-permute-start(bf16[128,2304]{1,0:T(8,128)(2,1)S(1)} %slice.539), channel_id=1, source_target_pairs={{0,1},{1,0},{2,3},{3,2},{4,5},{5,4},{6,7},{7,6},{8,9},{9,8},{10,11... | collective-permute-start | bytes 1769480 | tf_op jit(solution)/shard_map/ppermute | solution.py:73
  489.3 150.8 %collective-permute-start.121 = (bf16[288,2304]{1,0:T(8,128)(2,1)S(1)}, bf16[288,2304]{1,0:T(8,128)(2,1)S(1)}, u32[]{:S(2)}, u32[]{:S(2)}) collective-permute-start(bf16[288,2304]{1,0:T(8,128)(2,1)S(1)} %get-tuple-element.93), channel_id=1, source_target_pairs={{0,16},{8,24},{16,0},{24,8},{1,17},{9,25},{17,1},{25,9},{2,18},{10... | collective-permute-start | bytes 3981320 | tf_op jit(solution)/shard_map/ppermute | solution.py:138
  507.0 41.9 %collective-permute-start.122 = (bf16[288,2304]{1,0:T(8,128)(2,1)S(1)}, bf16[288,2304]{1,0:T(8,128)(2,1)S(1)}, u32[]{:S(2)}, u32[]{:S(2)}) collective-permute-start(bf16[288,2304]{1,0:T(8,128)(2,1)S(1)} %get-tuple-element.94), channel_id=1, source_target_pairs={{0,16},{8,24},{16,0},{24,8},{1,17},{9,25},{17,1},{25,9},{2,18},{10... | collective-permute-start | bytes 3981320 | tf_op jit(solution)/shard_map/ppermute | solution.py:138
  509.7 82.6 %collective-permute-start.113 = (bf16[288,2304]{1,0:T(8,128)(2,1)S(1)}, bf16[288,2304]{1,0:T(8,128)(2,1)S(1)}, u32[]{:S(2)}, u32[]{:S(2)}) collective-permute-start(bf16[288,2304]{1,0:T(8,128)(2,1)S(1)} %get-tuple-element.100), channel_id=1, source_target_pairs={{0,8},{8,0},{16,24},{24,16},{1,9},{9,1},{17,25},{25,17},{2,10},{10... | collective-permute-start | bytes 3981320 | tf_op jit(solution)/shard_map/ppermute | solution.py:138
  512.5 38.0 %collective-permute-start.85 = (bf16[128,2304]{1,0:T(8,128)(2,1)}, bf16[128,2304]{1,0:T(8,128)(2,1)S(1)}, u32[]{:S(2)}, u32[]{:S(2)}) collective-permute-start(bf16[128,2304]{1,0:T(8,128)(2,1)} %get-tuple-element.35), channel_id=1, source_target_pairs={{0,2},{1,3},{2,4},{3,5},{4,6},{5,7},{8,10},{9,11},{10,12},{11,13},... | collective-permute-start | bytes 1769480 | tf_op jit(solution)/shard_map/ppermute | solution.py:70
  589.3 166.8 %collective-permute-start.112 = (bf16[288,2304]{1,0:T(8,128)(2,1)S(1)}, bf16[288,2304]{1,0:T(8,128)(2,1)S(1)}, u32[]{:S(2)}, u32[]{:S(2)}) collective-permute-start(bf16[288,2304]{1,0:T(8,128)(2,1)S(1)} %get-tuple-element.99), channel_id=1, source_target_pairs={{0,8},{8,0},{16,24},{24,16},{1,9},{9,1},{17,25},{25,17},{2,10},{10... | collective-permute-start | bytes 3981320 | tf_op jit(solution)/shard_map/ppermute | solution.py:138
  589.4 44.6 %collective-permute-start.118 = (bf16[128,2304]{1,0:T(8,128)(2,1)S(1)}, bf16[128,2304]{1,0:T(8,128)(2,1)S(1)}, u32[]{:S(2)}, u32[]{:S(2)}) collective-permute-start(bf16[128,2304]{1,0:T(8,128)(2,1)S(1)} %get-tuple-element.97), channel_id=1, source_target_pairs={{0,8},{8,0},{16,24},{24,16},{1,9},{9,1},{17,25},{25,17},{2,10},{10... | collective-permute-start | bytes 1769480 | tf_op jit(solution)/shard_map/ppermute | solution.py:138
  591.5 16.7 %collective-permute-start.116 = (bf16[160,2304]{1,0:T(8,128)(2,1)S(1)}, bf16[160,2304]{1,0:T(8,128)(2,1)S(1)}, u32[]{:S(2)}, u32[]{:S(2)}) collective-permute-start(bf16[160,2304]{1,0:T(8,128)(2,1)S(1)} %get-tuple-element.96), channel_id=1, source_target_pairs={{0,16},{8,24},{16,0},{24,8},{1,17},{9,25},{17,1},{25,9},{2,18},{10... | collective-permute-start | bytes 2211848 | tf_op jit(solution)/shard_map/ppermute | solution.py:138
  592.3 70.2 %collective-permute-start.123 = (bf16[288,2304]{1,0:T(8,128)(2,1)S(1)}, bf16[288,2304]{1,0:T(8,128)(2,1)S(1)}, u32[]{:S(2)}, u32[]{:S(2)}) collective-permute-start(bf16[288,2304]{1,0:T(8,128)(2,1)S(1)} %add_convert_fusion), channel_id=1, source_target_pairs={{0,8},{8,0},{16,24},{24,16},{1,9},{9,1},{17,25},{25,17},{2,10},{10... | collective-permute-start | bytes 3981320 | tf_op jit(solution)/shard_map/ppermute | solution.py:138
  608.1 27.2 %collective-permute-start.120 = (bf16[128,2304]{1,0:T(8,128)(2,1)S(1)}, bf16[128,2304]{1,0:T(8,128)(2,1)S(1)}, u32[]{:S(2)}, u32[]{:S(2)}) collective-permute-start(bf16[128,2304]{1,0:T(8,128)(2,1)S(1)} %add_convert_fusion.4), channel_id=1, source_target_pairs={{0,16},{8,24},{16,0},{24,8},{1,17},{9,25},{17,1},{25,9},{2,18},{10... | collective-permute-start | bytes 1769480 | tf_op jit(solution)/shard_map/ppermute | solution.py:138
  640.1 27.1 %collective-permute-start.115 = (bf16[160,2304]{1,0:T(8,128)(2,1)S(1)}, bf16[160,2304]{1,0:T(8,128)(2,1)S(1)}, u32[]{:S(2)}, u32[]{:S(2)}) collective-permute-start(bf16[160,2304]{1,0:T(8,128)(2,1)S(1)} %get-tuple-element.95), channel_id=1, source_target_pairs={{0,16},{8,24},{16,0},{24,8},{1,17},{9,25},{17,1},{25,9},{2,18},{10... | collective-permute-start | bytes 2211848 | tf_op jit(solution)/shard_map/ppermute | solution.py:138
  649.9 23.2 %collective-permute-start.117 = (bf16[160,2304]{1,0:T(8,128)(2,1)S(1)}, bf16[160,2304]{1,0:T(8,128)(2,1)S(1)}, u32[]{:S(2)}, u32[]{:S(2)}) collective-permute-start(bf16[160,2304]{1,0:T(8,128)(2,1)S(1)} %add_convert_fusion.3), channel_id=1, source_target_pairs={{0,8},{8,0},{16,24},{24,16},{1,9},{9,1},{17,25},{25,17},{2,10},{10... | collective-permute-start | bytes 2211848 | tf_op jit(solution)/shard_map/ppermute | solution.py:138
  699.6 53.3 %collective-permute-start.100 = (bf16[4,4,72,1024]{3,2,1,0:T(8,128)(2,1)S(1)}, bf16[4,4,72,1024]{3,2,1,0:T(8,128)(2,1)S(1)}, u32[]{:S(2)}, u32[]{:S(2)}) collective-permute-start(bf16[4,4,72,1024]{3,2,1,0:T(8,128)(2,1)S(1)} %fusion.1), channel_id=1, source_target_pairs={{0,1},{1,0},{2,3},{3,2},{4,5},{5,4},{6,7},{7,6},{8,9},{9,8},{10,11... | collective-permute-start | bytes 7077896 | tf_op jit(solution)/shard_map/ppermute | solution.py:73
  711.5 46.6 %collective-permute-start.114 = (bf16[288,2304]{1,0:T(8,128)(2,1)S(1)}, bf16[288,2304]{1,0:T(8,128)(2,1)S(1)}, u32[]{:S(2)}, u32[]{:S(2)}) collective-permute-start(bf16[288,2304]{1,0:T(8,128)(2,1)S(1)} %add_convert_fusion.1), channel_id=1, source_target_pairs={{0,16},{8,24},{16,0},{24,8},{1,17},{9,25},{17,1},{25,9},{2,18},{10... | collective-permute-start | bytes 3981320 | tf_op jit(solution)/shard_map/ppermute | solution.py:138
  732.9 26.4 %collective-permute-start.111 = (bf16[64,2304]{1,0:T(8,128)(2,1)S(1)}, bf16[64,2304]{1,0:T(8,128)(2,1)S(1)}, u32[]{:S(2)}, u32[]{:S(2)}) collective-permute-start(bf16[64,2304]{1,0:T(8,128)(2,1)S(1)} %fusion.86), channel_id=1, source_target_pairs={{0,0},{1,4},{2,8},{3,12},{4,16},{5,20},{6,24},{7,28},{8,1},{9,5},{... | collective-permute-start | bytes 884744 | tf_op jit(solution)/shard_map/ppermute | solution.py:499
  733.9 30.8 %collective-permute-start.97 = (bf16[128,2304]{1,0:T(8,128)(2,1)S(1)}, bf16[128,2304]{1,0:T(8,128)(2,1)S(1)}, u32[]{:S(2)}, u32[]{:S(2)}) collective-permute-start(bf16[128,2304]{1,0:T(8,128)(2,1)S(1)} %get-tuple-element.101), channel_id=1, source_target_pairs={{0,2},{1,3},{2,4},{3,5},{4,6},{5,7},{8,10},{9,11},{10,12},{11,13},... | collective-permute-start | bytes 1769480 | tf_op jit(solution)/shard_map/ppermute | solution.py:70
  752.8 17.8 %collective-permute-start.99 = (bf16[128,2304]{1,0:T(8,128)(2,1)S(1)}, bf16[128,2304]{1,0:T(8,128)(2,1)S(1)}, u32[]{:S(2)}, u32[]{:S(2)}) collective-permute-start(bf16[128,2304]{1,0:T(8,128)(2,1)S(1)} %get-tuple-element.102), channel_id=1, source_target_pairs={{2,0},{3,1},{4,2},{5,3},{6,4},{7,5},{10,8},{11,9},{12,10},{13,11},... | collective-permute-start | bytes 1769480 | tf_op jit(solution)/shard_map/ppermute | solution.py:70
  758.1 26.2 %collective-permute-start.103 = (bf16[4,72,1024]{2,1,0:T(8,128)(2,1)S(1)}, bf16[4,72,1024]{2,1,0:T(8,128)(2,1)S(1)}, u32[]{:S(2)}, u32[]{:S(2)}) collective-permute-start(bf16[4,72,1024]{2,1,0:T(8,128)(2,1)S(1)} %get-tuple-element.108), channel_id=1, source_target_pairs={{0,24},{8,16},{16,8},{24,0},{1,25},{9,17},{17,9},{25,1},{2,26},{10... | collective-permute-start | bytes 1769480 | tf_op jit(solution)/shard_map/ppermute | solution.py:138
  759.3 26.6 %collective-permute-start.102 = (bf16[4,72,1024]{2,1,0:T(8,128)(2,1)S(1)}, bf16[4,72,1024]{2,1,0:T(8,128)(2,1)S(1)}, u32[]{:S(2)}, u32[]{:S(2)}) collective-permute-start(bf16[4,72,1024]{2,1,0:T(8,128)(2,1)S(1)} %get-tuple-element.109), channel_id=1, source_target_pairs={{0,16},{8,24},{16,0},{24,8},{1,17},{9,25},{17,1},{25,9},{2,18},{10... | collective-permute-start | bytes 1769480 | tf_op jit(solution)/shard_map/ppermute | solution.py:138
  786.6 18.8 %collective-permute-start.104 = (bf16[72,1024]{1,0:T(8,128)(2,1)S(1)}, bf16[72,1024]{1,0:T(8,128)(2,1)S(1)}, u32[]{:S(2)}, u32[]{:S(2)}) collective-permute-start(bf16[72,1024]{1,0:T(8,128)(2,1)S(1)} %get-tuple-element.133), channel_id=1, source_target_pairs={{2,0},{3,1},{4,2},{5,3},{6,4},{7,5},{0,6},{1,7},{10,8},{11,9},{12,... | collective-permute-start | bytes 442376 | tf_op jit(solution)/shard_map/ppermute | solution.py:125
  (175 other events, 1869.2 us)
